TPU v7x, 512 devices: a whole 4x8x8 slice. The times are simulated.
512 devices in a mesh: track: 64 (over y, z), cam: 8 (over x, core).
Axes of the slice: x: 4, y: 8, z: 8, core: 2. Of those that a mesh axis runs over, the one named last changes fastest.
Arguments:
- omega: bfloat16 [32, 9, 65536], P(None, None, ('track', 'cam')), may hold values from -6 to 6
- u_blocks: float32 [9, 9, 65536], P(None, None, ('track', 'cam')), may hold values from -5.4 to 36, as said below
- w_blocks: bfloat16 [9, 3, 262144], P(None, None, ('track', 'cam')), may hold values from -1.796875 to 1.796875
- v_inverse: float32 [3, 3, 65536], P(None, None, ('track', 'cam')), may hold values from -0.6 to 1.5, as said below
- obs_camera: int32 [262144], P(('track', 'cam')), may hold values from 0 to 65535, as said below
- obs_track: int32 [262144], P(('track', 'cam')), may hold values from 0 to 31, as said below
- obs_mask: int32 [262144], P(('track', 'cam')), may hold values from 0 to 1, as said below
Outputs:
- sketch: float32 [32, 9, 65536], P(None, None, ('track', 'cam'))
- basis: float32 [32, 9, 65536], P(None, None, ('track', 'cam'))
- factor: float32 [32, 32], replicated
Inputs may be any that keep to these rules, and one draw needn't show every extreme that they name: `obs_camera`: cameras c * 128 to (c + 1) * 128 - 1 belong to device c (track slower). Among one device's 512 observations, padding included, at most 2 name cameras of any one device, and exactly 2 name those of some device. `obs_track`: in each aligned block of 128 observations, slots 0 to 31 each hold one track of 2 to 4 consecutive observations from the block's start, in rising order; the padding after them carries slot 31. `obs_mask`: 1 on the observations of tracks, 0 on the padding at the end of each block. `u_blocks`: each block is symmetric. `v_inverse`: each block is symmetric positive definite.
All inputs are finite; a program needn't handle non-finite values.
Results may differ from a plain program's by a relative error of at most 0.00095.
Values may be sent and summed in bfloat16 or wider, within the bound.
No kernel may reach another device: no remote copies, remote signals or barrier semaphores. Data moves between devices by JAX's collectives and lax.ppermute only.
A program may use at most 64 MiB of HBM per device.

v0:
```python
import jax
import jax.numpy as jnp
from jax import lax
from jax.sharding import Mesh
from jax.sharding import PartitionSpec as P

BLK_OBS = 128
TRK_BLK = 32
TRACK = ("track_0", "track_1")
CAM = ("cam_0", "cam_1")
TRACK_CAM = ("track_0", "track_1", "cam_0", "cam_1")


HIGH = lax.Precision.HIGHEST


def cut_along(shard, dim, devices):
    lengths = shard.shape
    parts = shard.reshape(*lengths[:dim], devices, lengths[dim] // devices, *lengths[dim + 1 :])
    return jnp.moveaxis(parts, dim, 0)


def joined_along(parts, dim):
    lengths = list(parts.shape[1:])
    lengths[dim] *= parts.shape[0]
    return jnp.moveaxis(parts, 0, dim).reshape(lengths)


def joined_exchange(shard, axis, axes, splits, concats):
    sizes = [lax.axis_size(a) for a in axes]
    parts = cut_along(shard, splits[0], sizes[0])
    parts = jnp.moveaxis(cut_along(parts, splits[1] + 1, sizes[1]), 0, 1)
    inside = parts.shape[2:]
    parts = parts.reshape(-1, *inside)
    parts = lax.all_to_all(parts, axis, split_axis=0, concat_axis=0, tiled=True)
    parts = joined_along(parts.reshape(*sizes, *inside), concats[0] + 1)
    return joined_along(parts, concats[1])


def one_axis_at_a_time(shard, axes):
    for axis in axes:
        shard = lax.psum(shard, axis)
    return shard


def eliminate(gathered, w_blocks, v_inverse, obs_track, obs_mask):
    weights = w_blocks.astype(jnp.float32)
    live_mask = obs_mask.astype(jnp.float32)
    values = gathered.astype(jnp.float32)
    columns = values.shape[1]
    obs_count = values.shape[2]
    blocks = obs_count // BLK_OBS
    projected = (
        jnp.stack(
            [
                sum(
                    (
                        weights[comp_row, comp_col][None, :] * values[comp_row]
                        for comp_row in range(9)
                    )
                )
                for comp_col in range(3)
            ]
        )
        * live_mask
    )
    member = (
        obs_track.reshape(blocks, BLK_OBS)[:, :, None] == jnp.arange(TRK_BLK, dtype=jnp.int32)
    ).astype(jnp.float32)
    summed = jnp.einsum(
        "icbo,bot->icbt", projected.reshape(3, columns, blocks, BLK_OBS), member, precision=HIGH
    ).reshape(3, columns, blocks * TRK_BLK)
    solved = jnp.stack(
        [
            sum(
                (v_inverse[comp_row, comp_col][None, :] * summed[comp_col] for comp_col in range(3))
            )
            for comp_row in range(3)
        ]
    )
    spread = jnp.einsum(
        "icbt,bot->icbo", solved.reshape(3, columns, blocks, TRK_BLK), member, precision=HIGH
    ).reshape(3, columns, obs_count)
    returned = (
        jnp.stack(
            [
                sum(
                    (
                        weights[comp_row, comp_col][None, :] * spread[comp_col]
                        for comp_col in range(3)
                    )
                )
                for comp_row in range(9)
            ]
        )
        * live_mask
    )
    return returned.astype(jnp.bfloat16)


def on_device(omega, u_blocks, w_blocks, v_inverse, obs_camera, obs_track, obs_mask):
    track_count = lax.axis_size(TRACK)
    cam_count = lax.axis_size(CAM)
    devices = track_count * cam_count
    columns, params, cam_width = omega.shape
    obs_count = obs_camera.shape[0]
    capacity = max(2, 2 * obs_count // devices)
    buffer_slots = devices * capacity
    owner_index = obs_camera // cam_width
    ordering = jnp.argsort(owner_index, stable=True)
    ranked = owner_index[ordering]
    first_index = jnp.searchsorted(ranked, ranked, side="left")
    placed = ranked * capacity + jnp.arange(obs_count, dtype=jnp.int32) - first_index
    slot_index = jnp.zeros((obs_count,), jnp.int32).at[ordering].set(placed)
    request = (
        jnp.full((buffer_slots,), -1, jnp.int32)
        .at[slot_index]
        .set(obs_camera)
        .reshape(track_count, cam_count, capacity)
    )
    camera_ids = joined_exchange(request, TRACK_CAM, (TRACK, CAM), (0, 1), (0, 1))
    table_start = (lax.axis_index(TRACK) * cam_count + lax.axis_index(CAM)) * cam_width
    table_width = omega.shape[2]
    is_live = camera_ids >= 0
    local_ids = jnp.where(is_live, camera_ids - table_start, 0).reshape(-1)
    gathered_rows = jnp.take(omega, local_ids, axis=2)
    outgoing = (
        gathered_rows.reshape(columns, params, track_count, cam_count, capacity)
        .transpose(2, 3, 1, 4, 0)
        .reshape(track_count, cam_count, params, capacity * columns)
    )
    returned = joined_exchange(outgoing, TRACK_CAM, (TRACK, CAM), (0, 1), (0, 1))
    received = (
        returned.reshape(track_count, cam_count, params, capacity, columns)
        .transpose(2, 4, 0, 1, 3)
        .reshape(params, columns, buffer_slots)
    )
    needed = jnp.take(received, slot_index, axis=2)
    contribution = eliminate(needed, w_blocks, v_inverse, obs_track, obs_mask)
    buffer = (
        jnp.zeros((params, columns, buffer_slots), jnp.bfloat16)
        .at[:, :, slot_index]
        .set(contribution)
    )
    packed = (
        buffer.reshape(params, columns, track_count, cam_count, capacity)
        .transpose(2, 3, 0, 4, 1)
        .reshape(track_count, cam_count, params, capacity * columns)
    )
    arrived = lax.all_to_all(
        lax.all_to_all(packed, CAM, split_axis=1, concat_axis=1, tiled=True),
        TRACK,
        split_axis=0,
        concat_axis=0,
        tiled=True,
    )
    terms = (
        arrived.reshape(track_count, cam_count, params, capacity, columns)
        .transpose(4, 2, 0, 1, 3)
        .reshape(columns, params, buffer_slots)
        .astype(jnp.float32)
    )
    target = jnp.where(is_live, camera_ids - table_start, table_width).reshape(-1)
    incoming = (
        jnp.zeros((columns, params, table_width + 1), jnp.float32)
        .at[:, :, target]
        .add(terms)[:, :, :table_width]
    )
    own_term = jnp.einsum("mnk,jnk->jmk", u_blocks, omega.astype(jnp.float32), precision=HIGH)
    sketch = own_term - incoming
    flat_rows = sketch.reshape(columns, params * cam_width)
    gram_local = jnp.dot(flat_rows, flat_rows.T, precision=HIGH, preferred_element_type=jnp.float32)
    row_total = params * cam_width * devices
    lower_factor = jnp.linalg.cholesky(one_axis_at_a_time(gram_local, TRACK_CAM) / row_total)
    basis_rows = jax.scipy.linalg.solve_triangular(lower_factor, flat_rows, lower=True).reshape(
        sketch.shape
    )
    return (sketch, basis_rows, lower_factor.T)


def solution(mesh):
    split = Mesh(mesh.devices.reshape(8, 8, 4, 2), ("track_0", "track_1", "cam_0", "cam_1"))
    return jax.shard_map(
        on_device,
        mesh=split,
        in_specs=(
            P(None, None, TRACK_CAM),
            P(None, None, TRACK_CAM),
            P(None, None, TRACK_CAM),
            P(None, None, TRACK_CAM),
            P(TRACK_CAM),
            P(TRACK_CAM),
            P(TRACK_CAM),
        ),
        out_specs=(P(None, None, TRACK_CAM), P(None, None, TRACK_CAM), P()),
        check_vma=False,
    )
```

profile of v0, /device:TPU:1, one launch (start us, length us, event | category | flops | bytes accessed | tf_op | source)
XLA Modules:
  0.0 457.0 jit_solution(17015729782735727889)
XLA Ops:
  0.6 0.7 add_select_fusion
  1.3 3.8 sort.17
  5.1 3.5 gather_fusion.1
  8.6 35.9 %while.25 = (s32[]{:T(128)}, u32[512]{0:T(512)S(1)}, u32[512]{0:T(512)S(1)}, s32[512]{0:T(512)S(1)}, s32[]{:T(128)}, /*index=5*/s32[]{:T(128)}, s32[]{}) while((s32[]{:T(128)}, u32[512]{0:T(512)S(1)}, u32[512]{0:T(512)S(1)}, s32[512]{0:T(512)S(1)}, s32[]{:T(128)}, /*index=5*/s32[]{:T(128)}, s32[]{}) %tuple.88), condition=%wide.region_2.3_spmd.clone, body=%wide.region_1.2_spmd.clone.sunk | while | flops 10244 | bytes 40037 | solution.py:112
  8.7 3.5 gather_fusion
  12.3 3.5 gather_fusion
  15.9 3.5 gather_fusion
  19.4 3.5 gather_fusion
  23.0 3.5 gather_fusion
  26.6 3.5 gather_fusion
  30.2 3.5 gather_fusion
  33.8 3.5 gather_fusion
  37.4 3.5 gather_fusion
  41.0 3.5 gather_fusion
  44.5 2.4 scatter_custom_fusion
  47.0 2.6 scatter_custom_fusion.1
  49.6 0.9 reshape_transpose_transpose_reshape_reshape_reshape.6
  50.5 22.2 %all-to-all-start = ((s32[512,1,1,2]{3,2,1,0:T(1,128)}), s32[512,1,1,2]{3,2,1,0:T(1,128)S(1)}, u32[]{:S(2)}, u32[]{:S(2)}) async-start(s32[512,1,1,2]{3,2,1,0:T(1,128)} %bitcast.1), calls=%async_computation | async-start | bytes 524288 | tf_op jit(solution)/shard_map/all_to_all | solution.py:35
  73.2 16.9 %all-to-all-done = s32[512,1,1,2]{3,2,1,0:T(1,128)S(1)} async-done(((s32[512,1,1,2]{3,2,1,0:T(1,128)}), s32[512,1,1,2]{3,2,1,0:T(1,128)S(1)}, u32[]{:S(2)}, u32[]{:S(2)}) %all-to-all-start) | async-done | bytes 4128 | tf_op jit(solution)/shard_map/all_to_all | solution.py:35
  90.1 1.1 compare_select_fusion.2
  92.0 8.4 %gather_fusion.2 = bf16[1024,32,9]{1,2,0:T(8,128)(2,1)} fusion(bf16[32,9,128]{0,1,2:T(8,128)(2,1)S(1)} %copy.329, s32[1024]{0:T(1024)S(1)} %get-tuple-element.168), kind=kCustom, calls=%fused_computation.2 | custom fusion | bytes 1183744 | tf_op jit(solution)/shard_map/jit(_take)/gather | solution.py:126
  100.4 2.8 copy.333
  103.3 2.7 fusion
  106.0 2.2 reshape_transpose_transpose_reshape_reshape_reshape.7
  108.2 2.1 copy.334
  110.4 2.5 reshape.1603
  112.9 8.6 %all-to-all-start.1 = ((bf16[512,2,288]{2,1,0:T(2,128)(2,1)}), bf16[512,2,288]{2,1,0:T(2,128)(2,1)S(1)}, u32[]{:S(2)}, u32[]{:S(2)}) async-start(bf16[512,2,288]{2,1,0:T(2,128)(2,1)} %reshape.1603), calls=%async_computation.1 | async-start | bytes 1572864 | tf_op jit(solution)/shard_map/all_to_all | solution.py:35
  125.5 0.7 mul.901
  126.1 0.7 mul.904
  128.7 20.0 %all-to-all-done.1 = bf16[512,2,288]{2,1,0:T(2,128)(2,1)S(1)} async-done(((bf16[512,2,288]{2,1,0:T(2,128)(2,1)}), bf16[512,2,288]{2,1,0:T(2,128)(2,1)S(1)}, u32[]{:S(2)}, u32[]{:S(2)}) %all-to-all-start.1) | async-done | bytes 589856 | tf_op jit(solution)/shard_map/all_to_all | solution.py:35
  148.7 1.6 reshape.1604
  150.3 1.3 copy.437
  151.6 2.7 copy.336
  154.3 5.4 %copy.337 = bf16[9,32,64,8,2]{1,4,3,2,0:T(2,128)(2,1)S(1)} copy(bf16[9,32,64,8,2]{2,1,4,0,3:T(8,128)(2,1)} %bitcast.196) | data formatting | bytes 1179648 | tf_op jit(solution)/shard_map/transpose | solution.py:135
  159.8 3.7 copy.338
  163.4 3.4 gather_fusion.3
  166.8 1.2 copy.339
  170.4 2.0 copy.374
  172.4 2.5 broadcast_in_dim.76
  174.9 47.4 %scatter_fusion = bf16[9,32,1024]{1,0,2:T(8,128)(2,1)} fusion(bf16[9,32,1024]{1,0,2:T(8,128)(2,1)} %broadcast_in_dim.76, s32[512]{0:T(512)S(1)} %copy-done.6, bf16[512,9,32]{2,1,0:T(8,128)(2,1)S(1)} %copy.374), kind=kCustom, calls=%fused_computation.6 | custom fusion | bytes 886784 | tf_op jit(solution)/shard_map/scatter | solution.py:143
  222.3 4.5 copy.375
  226.8 0.8 reshape.1605
  227.6 13.7 %all_to_all.20 = bf16[8,2,18432]{2,1,0:T(2,128)(2,1)S(1)} all-to-all(bf16[8,2,18432]{2,1,0:T(2,128)(2,1)S(1)} %reshape.1605), channel_id=1, replica_groups=mesh['track_0'=8,'track_1'=8,'cam_0'=4,'cam_1'=2] {'cam_0','cam_1'}, dimensions={0} | all-to-all | bytes 1179648 | tf_op jit(solution)/shard_map/all_to_all | solution.py:151
  241.3 0.7 reshape.1606
  242.1 1.2 copy.376
  243.3 1.5 reshape.1607
  244.9 5.5 %all-to-all-start.3 = ((bf16[64,2,2304]{2,1,0:T(2,128)(2,1)}), bf16[64,2,2304]{2,1,0:T(2,128)(2,1)S(1)}, u32[]{:S(2)}, u32[]{:S(2)}) async-start(bf16[64,2,2304]{2,1,0:T(2,128)(2,1)} %reshape.1607), calls=%async_computation.3 | async-start | bytes 1179648 | tf_op jit(solution)/shard_map/all_to_all | solution.py:150
  250.4 1.4 copy.330
  252.0 15.8 %all-to-all-done.3 = bf16[64,2,2304]{2,1,0:T(2,128)(2,1)S(1)} async-done(((bf16[64,2,2304]{2,1,0:T(2,128)(2,1)}), bf16[64,2,2304]{2,1,0:T(2,128)(2,1)S(1)}, u32[]{:S(2)}, u32[]{:S(2)}) %all-to-all-start.3) | async-done | bytes 589856 | tf_op jit(solution)/shard_map/all_to_all | solution.py:150
  267.8 0.7 reshape.1608
  268.5 1.9 copy.377
  270.5 1.6 convert_bitcast_fusion
  272.1 4.8 %copy.378 = f32[32,9,64,8,2]{0,4,3,2,1:T(2,128)} copy(f32[32,9,64,8,2]{2,0,4,1,3:T(8,128)S(1)} %convert_bitcast_fusion) | data formatting | bytes 2359296 | tf_op jit(solution)/shard_map/convert_element_type | solution.py:161
  276.9 8.5 %copy.379 = f32[1024,32,9]{1,2,0:T(8,128)} copy(f32[1024,32,9]{1,0,2:T(8,128)} %bitcast.163) | data formatting | bytes 2359296 | tf_op jit(solution)/shard_map/convert_element_type | solution.py:161
  285.4 80.9 %scatter_fusion.1 = f32[32,9,129]{0,1,2:T(8,128)S(1)} fusion(f32[32,9,129]{0,1,2:T(8,128)S(1)} %broadcast_in_dim.69, s32[1024]{0:T(1024)S(1)} %bitcast.263, f32[1024,32,9]{1,2,0:T(8,128)} %copy.379), kind=kCustom, calls=%fused_computation.7 | custom fusion | flops 294912 | bytes 3543040 | tf_op jit(solution)/shard_map/scatter-add | solution.py:167
  366.3 1.9 fusion.1
  369.3 23.3 %psum.28 = f32[32,32]{0,1:T(8,128)S(1)} all-reduce(f32[32,32]{0,1:T(8,128)S(1)} %convolution_bitcast_fusion.2), channel_id=1, replica_groups=mesh['track_0'=8,'track_1'=8,'cam_0'=4,'cam_1'=2] {'track_0'}, use_global_device_ids=true, to_apply=%region_7.8 | all-reduce | flops 1024 | bytes 8192 | tf_op jit(solution)/shard_map/psum | solution.py:42
  392.5 20.2 %psum.29 = f32[32,32]{0,1:T(8,128)S(1)} all-reduce(f32[32,32]{0,1:T(8,128)S(1)} %psum.28), channel_id=1, replica_groups=mesh['track_0'=8,'track_1'=8,'cam_0'=4,'cam_1'=2] {'track_1'}, use_global_device_ids=true, to_apply=%region_8.9 | all-reduce | flops 1024 | bytes 8192 | tf_op jit(solution)/shard_map/psum | solution.py:42
  412.8 11.6 %psum.30 = f32[32,32]{0,1:T(8,128)S(1)} all-reduce(f32[32,32]{0,1:T(8,128)S(1)} %psum.29), channel_id=1, replica_groups=mesh['track_0'=8,'track_1'=8,'cam_0'=4,'cam_1'=2] {'cam_0'}, use_global_device_ids=true, to_apply=%region_9.10 | all-reduce | flops 1024 | bytes 8192 | tf_op jit(solution)/shard_map/psum | solution.py:42
  424.4 24.2 %psum.31 = f32[32,32]{0,1:T(8,128)S(1)} all-reduce(f32[32,32]{0,1:T(8,128)S(1)} %psum.30), channel_id=1, replica_groups=mesh['track_0'=8,'track_1'=8,'cam_0'=4,'cam_1'=2] {'cam_1'}, use_global_device_ids=true, to_apply=%region_10.11 | all-reduce | flops 1024 | bytes 8192 | tf_op jit(solution)/shard_map/psum | solution.py:42
  448.6 2.9 cholesky.16
  452.9 2.4 custom-call.7
  455.3 0.7 copy.388
  456.0 1.0 fusion.7
  (155 shorter events, 12.4 us)
Async XLA Ops:
  8.6 64.1 %copy-start.3 = (bf16[32,9,128]{2,0,1:T(8,128)(2,1)S(1)}, bf16[32,9,128]{2,0,1:T(8,128)(2,1)}, u32[]{:S(2)}) copy-start(bf16[32,9,128]{2,0,1:T(8,128)(2,1)} %param.9) | copy-start | bytes 221188
  47.0 53.4 %copy-start.5 = (s32[512]{0:T(512)}, s32[512]{0:T(512)S(1)}, u32[]{:S(2)}) copy-start(s32[512]{0:T(512)S(1)} %compare_select_fusion.5) | copy-start | bytes 6148
  50.5 39.6 %all-to-all-start = ((s32[512,1,1,2]{3,2,1,0:T(1,128)}), s32[512,1,1,2]{3,2,1,0:T(1,128)S(1)}, u32[]{:S(2)}, u32[]{:S(2)}) async-start(s32[512,1,1,2]{3,2,1,0:T(1,128)} %bitcast.1), calls=%async_computation | async-start | bytes 524288 | tf_op jit(solution)/shard_map/all_to_all | solution.py:35
  110.4 11.1 %copy-start.20 = (f32[3,3,128]{2,1,0:T(4,128)S(1)}, f32[3,3,128]{2,1,0:T(4,128)}, u32[]{:S(2)}) copy-start(f32[3,3,128]{2,1,0:T(4,128)} %param.12) | copy-start | bytes 13828
  110.4 17.6 %copy-start.22 = (s32[512]{0:T(512)S(1)}, s32[512]{0:T(512)}, u32[]{:S(2)}) copy-start(s32[512]{0:T(512)} %param.15) | copy-start | bytes 6148
  110.4 18.2 %copy-start.2 = (bf16[9,3,512]{2,1,0:T(4,128)(2,1)S(1)}, bf16[9,3,512]{2,1,0:T(4,128)(2,1)}, u32[]{:S(2)}) copy-start(bf16[9,3,512]{2,1,0:T(4,128)(2,1)} %param.11) | copy-start | bytes 82948
  112.9 35.8 %all-to-all-start.1 = ((bf16[512,2,288]{2,1,0:T(2,128)(2,1)}), bf16[512,2,288]{2,1,0:T(2,128)(2,1)S(1)}, u32[]{:S(2)}, u32[]{:S(2)}) async-start(bf16[512,2,288]{2,1,0:T(2,128)(2,1)} %reshape.1603), calls=%async_computation.1 | async-start | bytes 1572864 | tf_op jit(solution)/shard_map/all_to_all | solution.py:35
  159.8 3.7 copy-start.7
  163.4 4.6 %copy-start.21 = (pred[512]{0:T(512)(128)(4,1)S(1)}, pred[512]{0:T(512)(128)(4,1)}, u32[]{:S(2)}) copy-start(pred[512]{0:T(512)(128)(4,1)} %compare_and_fusion.1) | copy-start | bytes 1540
  168.0 0.7 copy-start.8
  168.1 0.7 copy-start.10
  168.1 1.1 copy-start.11
  168.1 1.1 copy-start.12
  168.1 1.1 copy-start.13
  168.1 1.1 copy-start.14
  168.1 1.1 copy-start.15
  168.1 1.1 copy-start.16
  168.1 1.1 copy-start.17
  168.1 1.1 copy-start.18
  168.1 1.1 copy-start.19
  169.6 0.8 copy-start.9
  172.4 2.5 copy-start.6
  242.1 8.3 %copy-start.4 = (f32[9,9,128]{2,1,0:T(8,128)S(1)}, f32[9,9,128]{2,1,0:T(8,128)}, u32[]{:S(2)}) copy-start(f32[9,9,128]{2,1,0:T(8,128)} %param.10) | copy-start | bytes 124420
  243.3 8.5 %copy-start.1 = (s32[512,1,1,2]{3,2,1,0:T(1,128)S(1)}, s32[512,1,1,2]{3,2,1,0:T(1,128)}, u32[]{:S(2)}) copy-start(s32[512,1,1,2]{3,2,1,0:T(1,128)} %get-tuple-element.129) | copy-start | bytes 12292
  244.9 23.0 %all-to-all-start.3 = ((bf16[64,2,2304]{2,1,0:T(2,128)(2,1)}), bf16[64,2,2304]{2,1,0:T(2,128)(2,1)S(1)}, u32[]{:S(2)}, u32[]{:S(2)}) async-start(bf16[64,2,2304]{2,1,0:T(2,128)(2,1)} %reshape.1607), calls=%async_computation.3 | async-start | bytes 1179648 | tf_op jit(solution)/shard_map/all_to_all | solution.py:150
  368.5 88.5 %copy-start = (f32[32,9,128]{2,0,1:T(8,128)}, f32[32,9,128]{2,0,1:T(8,128)S(1)}, u32[]{:S(2)}) copy-start(f32[32,9,128]{2,0,1:T(8,128)S(1)} %copy.387) | copy-start | bytes 442372
where the time goes:
time: 460 us; the launch traced here: 457 us
  local copies, waits for them, and re-layouts  169 us (37%)
  other arithmetic  100 us (22%)
  blocking collectives  93 us (20%)
  waiting for transfers between devices  52.7 us (11%)
  starting transfers between devices  36.2 us (8%)
    scatter-add x1, other arithmetic, on_device(): incoming = jnp.zeros((columns, params, table_width + 1), jnp.float32).at[...  80.9 us
    psum x4, blocking collectives, one_axis_at_a_time(): shard = lax.psum(shard, axis)  79.3 us
    scatter x1, local copies, waits for them, and re-layouts, on_device(): buffer = jnp.zeros((params, columns, buffer_slots), jnp.bfloat16).at[:, :...  47.4 us
    all_to_all x2, waiting for transfers between devices, joined_exchange(): parts = lax.all_to_all(parts, axis, split_axis=0, concat_axis=0, tiled=True)  36.9 us
    gather x10, local copies, waits for them, and re-layouts, on_device(): first_index = jnp.searchsorted(ranked, ranked, side='left')  34.9 us
    all_to_all x2, starting transfers between devices, joined_exchange(): parts = lax.all_to_all(parts, axis, split_axis=0, concat_axis=0, tiled=True)  30.7 us
    all_to_all x1, waiting for transfers between devices, on_device(): lax.all_to_all(lax.all_to_all(packed, CAM, split_axis=1, concat_axis=1, t...  15.8 us
    all_to_all x1, blocking collectives, on_device(): lax.all_to_all(packed, CAM, split_axis=1, concat_axis=1, tiled=True)  13.7 us
  transfers between devices with their start and end apart: 3, of which 3 were waited for; matrix products, arithmetic and copies ran while one was open for 2% of the time, Pallas kernels for 0%

commit v1 on v0

v1 whole, which is shorter than its diff:
```python
import functools

import jax
import jax.numpy as jnp
from jax import lax
from jax.experimental import pallas as pl
from jax.experimental.pallas import tpu as pltpu
from jax.sharding import Mesh
from jax.sharding import PartitionSpec as P

BLK_OBS = 128
TRK_BLK = 32
LANES = 128
PARAMS = 9
COLS = 32
TRACK = ("track_0", "track_1")
CAM = ("cam_0", "cam_1")
TRACK_CAM = TRACK + CAM
HIGH = lax.Precision.HIGHEST
F32 = jnp.float32
BF16 = jnp.bfloat16


def dot_lanes(lhs, rhs):
    return lax.dot_general(lhs, rhs, (((1,), (1,)), ((), ())), preferred_element_type=F32)


def call(kernel, shapes, *args, scratch=()):
    return pl.pallas_call(
        kernel,
        out_shape=tuple(jax.ShapeDtypeStruct(s, d) for s, d in shapes),
        scratch_shapes=list(scratch),
        compiler_params=pltpu.CompilerParams(vmem_limit_bytes=48 << 20),
    )(*args)


def request_kernel(capacity, camera_ref, mask_ref, w_ref, request_ref, slot_ref, rows):
    obs = camera_ref.shape[1]
    camera = camera_ref[...]
    owner = lax.shift_right_logical(camera, 7)
    owner_f = owner.astype(F32)
    blocks = obs // LANES
    sub = lax.broadcasted_iota(jnp.int32, (LANES, LANES), 0)
    lane = lax.broadcasted_iota(jnp.int32, (LANES, LANES), 1)
    row_of = [owner_f[:, LANES * b : LANES * (b + 1)] for b in range(blocks)]
    column_of = [jnp.broadcast_to(r, (LANES, LANES)).T for r in row_of]
    ranks = []
    for q in range(blocks):
        same = jnp.where((column_of[q] == row_of[q]) & (sub < lane), 1.0, 0.0)
        for b in range(q):
            same = same + jnp.where(column_of[b] == row_of[q], 1.0, 0.0)
        ranks.append(jnp.sum(same, axis=0, keepdims=True))
    slot = owner * capacity + jnp.concatenate(ranks, axis=1).astype(jnp.int32)
    slot_ref[...] = slot
    live = mask_ref[...].astype(F32)
    rows[...] = jnp.zeros(rows.shape, F32)
    for m in range(PARAMS):
        rows[3 * m : 3 * m + 3, :] = w_ref[m].astype(F32) * live
    rows[3 * PARAMS : 3 * PARAMS + 1, :] = (camera & (LANES - 1)).astype(F32)
    values = rows[...].astype(BF16)
    slots = request_ref.shape[0]
    step = 256
    for s in range(0, slots, step):
        ids = lax.broadcasted_iota(jnp.int32, (step, obs), 0) + s
        chosen = jnp.where(ids == slot, 1.0, 0.0).astype(BF16)
        request_ref[s : s + step, :] = dot_lanes(chosen, values).astype(BF16)


def member_kernel(slot_ref, track_ref, by_track_ref, by_slot_ref):
    obs = slot_ref.shape[1]
    tracks, slots = by_track_ref.shape
    position = lax.broadcasted_iota(jnp.int32, (1, obs), 1)
    track = lax.shift_right_logical(position, 7) * TRK_BLK + track_ref[...]
    ids = lax.broadcasted_iota(jnp.int32, (tracks, obs), 0)
    member = jnp.where(ids == track, 1.0, 0.0).astype(BF16)
    step = 256
    for s in range(0, slots, step):
        ids = lax.broadcasted_iota(jnp.int32, (step, obs), 0) + s
        chosen = jnp.where(ids == slot_ref[...], 1.0, 0.0).astype(BF16)
        by_track_ref[:, s : s + step] = dot_lanes(member, chosen).astype(BF16)
        by_slot_ref[s : s + step, :] = dot_lanes(chosen, member).astype(BF16)


def spread_of(width):
    row = lax.broadcasted_iota(jnp.int32, (LANES, width), 0)
    lane = lax.broadcasted_iota(jnp.int32, (LANES, width), 1)
    third = lax.shift_right_logical(lane & (LANES - 1), 5)
    wanted = 3 * lax.shift_right_logical(lane, 7) + third
    return jnp.where((row == wanted) & (third < 3), 1.0, 0.0).astype(BF16)


def row_everywhere(index):
    row = lax.broadcasted_iota(jnp.int32, (LANES, LANES), 0)
    return jnp.where(row == index, 1.0, 0.0).astype(BF16)


def dot(lhs, rhs):
    return jnp.dot(lhs, rhs, preferred_element_type=F32)


def camera_onehot(request):
    local = dot(request, row_everywhere(3 * PARAMS))
    lane = lax.broadcasted_iota(jnp.int32, local.shape, 1).astype(F32)
    return local == lane


def project_kernel(request_ref, table_ref, reply_ref):
    spread = spread_of(PARAMS * LANES)
    step = 256
    for s in range(0, request_ref.shape[0], step):
        request = request_ref[s : s + step, :]
        chosen = jnp.where(camera_onehot(request), 1.0, 0.0).astype(BF16)
        total = jnp.zeros((step, LANES), F32)
        for m in range(PARAMS):
            block = slice(LANES * m, LANES * (m + 1))
            total = total + dot_lanes(chosen, table_ref[block, :]) * dot(request, spread[:, block])
        reply_ref[s : s + step, :] = total.astype(BF16)


def solve_kernel(reply_ref, by_track_ref, by_slot_ref, v_ref, out_ref):
    summed = dot(by_track_ref[...], reply_ref[...]).T
    parts = []
    for i in range(3):
        part = jnp.zeros((COLS, LANES), F32)
        for k in range(3):
            part = part + v_ref[i, k : k + 1, :] * summed[COLS * k : COLS * (k + 1), :]
        parts.append(part)
    parts.append(jnp.zeros((LANES - 3 * COLS, LANES), F32))
    solved = jnp.concatenate(parts, axis=0).astype(BF16)
    out_ref[...] = dot_lanes(by_slot_ref[...], solved).astype(BF16)


def weights_kernel(request_ref, omega_ref, u_ref, weights_ref, own_ref):
    slots = request_ref.shape[0]
    step = 256
    for s in range(0, slots, step):
        request = request_ref[s : s + step, :]
        chosen = camera_onehot(request)
        for i in range(3):
            for m in range(PARAMS):
                spread = dot(request, row_everywhere(3 * m + i))
                weights_ref[i * slots + s : i * slots + s + step, LANES * m : LANES * (m + 1)] = (
                    jnp.where(chosen, spread, 0.0).astype(BF16)
                )
    table = [omega_ref[n].astype(F32) for n in range(PARAMS)]
    for m in range(PARAMS):
        total = jnp.zeros((COLS, LANES), F32)
        for n in range(PARAMS):
            total = total + u_ref[m, n : n + 1, :] * table[n]
        own_ref[:, LANES * m : LANES * (m + 1)] = total


def sketch_kernel(solved_ref, weights_ref, own_ref, sketch_ref, gram_ref):
    slots = solved_ref.shape[0]
    turned = solved_ref[...].astype(F32).T.astype(BF16)
    sketch = own_ref[...]
    for i in range(3):
        sketch = sketch - dot(
            turned[COLS * i : COLS * (i + 1), :], weights_ref[i * slots : (i + 1) * slots, :]
        )
    sketch_ref[...] = sketch
    gram = lax.dot_general(
        sketch, sketch, (((1,), (1,)), ((), ())), precision=HIGH, preferred_element_type=F32
    )
    packed = jnp.concatenate([gram[8 * q : 8 * q + 8, :] for q in range(4)], axis=1)
    gram_ref[...] = jnp.broadcast_to(packed[None], gram_ref.shape)


def gather_kernel(parts_ref, out_ref):
    out_ref[...] = jnp.broadcast_to(jnp.sum(parts_ref[...], axis=0)[None], out_ref.shape)


def finish_kernel(row_total, parts_ref, sketch_ref, basis_ref, factor_ref):
    packed = jnp.sum(parts_ref[...], axis=0) / row_total
    gram = jnp.concatenate([packed[:, COLS * q : COLS * (q + 1)] for q in range(4)], axis=0)
    row = lax.broadcasted_iota(jnp.int32, (COLS, COLS), 0)
    column = lax.broadcasted_iota(jnp.int32, (COLS, COLS), 1)
    work = jnp.concatenate([gram, jnp.where(row == column, 1.0, 0.0)], axis=1)
    wide_row = lax.broadcasted_iota(jnp.int32, work.shape, 0)
    for k in range(COLS):
        pivot = work[k : k + 1, k : k + 1]
        scale = 1.0 / jnp.sqrt(pivot)
        scaled = work[k : k + 1, :] * scale
        below = work[:, k : k + 1] * scale
        work = jnp.where(
            wide_row > k, work - below * scaled, jnp.where(wide_row == k, scaled, work)
        )
    factor_ref[...] = jnp.where(column >= row, work[:, :COLS], 0.0)
    basis_ref[...] = jnp.dot(
        work[:, COLS:], sketch_ref[...], precision=HIGH, preferred_element_type=F32
    )


def exchange(values, axes, capacity):
    slots = values.shape[0]
    parts = values.reshape(slots // capacity, capacity, LANES)
    parts = lax.all_to_all(parts, axes, split_axis=0, concat_axis=0, tiled=True)
    return parts.reshape(slots, LANES)


def on_device(omega, u_blocks, w_blocks, v_inverse, obs_camera, obs_track, obs_mask):
    track_count = lax.axis_size(TRACK)
    cam_count = lax.axis_size(CAM)
    devices = track_count * cam_count
    columns, params, cam_width = omega.shape
    obs = obs_camera.shape[0]
    capacity = max(2, 2 * obs // devices)
    slots = devices * capacity
    tracks = obs // BLK_OBS * TRK_BLK

    request, slot = call(
        functools.partial(request_kernel, capacity),
        (((slots, LANES), BF16), ((1, obs), jnp.int32)),
        obs_camera.reshape(1, obs),
        obs_mask.reshape(1, obs),
        w_blocks,
        scratch=(pltpu.VMEM((LANES, obs), F32),),
    )
    asked = exchange(request, TRACK_CAM, capacity)

    table = omega.transpose(1, 0, 2)
    wide_table = jnp.concatenate(
        [table, table, table, jnp.zeros((params, LANES - 3 * columns, cam_width), BF16)], axis=1
    ).reshape(params * LANES, cam_width)
    (reply,) = call(project_kernel, (((slots, LANES), BF16),), asked, wide_table)
    projected = exchange(reply, TRACK_CAM, capacity)

    by_track, by_slot = call(
        member_kernel,
        (((tracks, slots), BF16), ((slots, tracks), BF16)),
        slot,
        obs_track.reshape(1, obs),
    )
    (outgoing,) = call(
        solve_kernel, (((slots, LANES), BF16),), projected, by_track, by_slot, v_inverse
    )
    solved = exchange(outgoing, TRACK_CAM, capacity)

    weights, own = call(
        weights_kernel,
        (((3 * slots, params * cam_width), BF16), ((columns, params * cam_width), F32)),
        asked,
        table,
        u_blocks,
    )
    sketch, gram = call(
        sketch_kernel,
        (((columns, params * cam_width), F32), ((cam_count, 8, LANES), F32)),
        solved,
        weights,
        own,
    )
    gram = lax.all_to_all(gram, CAM, split_axis=0, concat_axis=0, tiled=True)
    (gram,) = call(gather_kernel, (((track_count, 8, LANES), F32),), gram)
    gram = lax.all_to_all(gram, TRACK, split_axis=0, concat_axis=0, tiled=True)
    basis, factor = call(
        functools.partial(finish_kernel, float(params * cam_width * devices)),
        (((columns, params * cam_width), F32), ((columns, columns), F32)),
        gram,
        sketch,
    )
    shape = (columns, params, cam_width)
    return (sketch.reshape(shape), basis.reshape(shape), factor)


def solution(mesh):
    track, cam = mesh.devices.shape
    split = Mesh(
        mesh.devices.reshape(8, track // 8, cam // 2, 2), ("track_0", "track_1", "cam_0", "cam_1")
    )
    return jax.shard_map(
        on_device,
        mesh=split,
        in_specs=(
            P(None, None, TRACK_CAM),
            P(None, None, TRACK_CAM),
            P(None, None, TRACK_CAM),
            P(None, None, TRACK_CAM),
            P(TRACK_CAM),
            P(TRACK_CAM),
            P(TRACK_CAM),
        ),
        out_specs=(P(None, None, TRACK_CAM), P(None, None, TRACK_CAM), P()),
        check_vma=False,
    )
```

time: 460 us -> 136 us (0.30)
  local copies, waits for them, and re-layouts: 169 us -> 6.68 us
  other arithmetic: 100 us -> 1.12 us
  blocking collectives: 93 us -> 7.72 us
  Pallas kernels: 0 us -> 19.6 us
  starting transfers between devices: 36.2 us -> 44.3 us
    scatter-add x1 -> x0, other arithmetic: 80.9 us -> none  [on_device(): incoming = jnp.zeros((columns, params, table_width + 1), jnp.float32).at[...]
    psum x4 -> x0, blocking collectives: 79.3 us -> none  [one_axis_at_a_time(): shard = lax.psum(shard, axis)]
    gather x15 -> x0, local copies, waits for them, and re-layouts: 54.2 us -> none  [the longest x10 34.9 us: on_device(): first_index = jnp.searchsorted(ranked, ranked, side='left')]
    scatter x3 -> x0, local copies, waits for them, and re-layouts: 52.4 us -> none  [the longest x1 47.4 us: on_device(): buffer = jnp.zeros((params, columns, buffer_slots), jnp.bfloat16).at[:, :...]
    pallas_call x0 -> x8, Pallas kernels: none -> 19.6 us  [call(): pl.pallas_call(kernel, out_shape=tuple((jax.ShapeDtypeStruct(s, d) for s,...]
    convert_element_type x3 -> x0, local copies, waits for them, and re-layouts: 15.3 us -> none  [the longest x2 13.3 us: on_device(): terms = arrived.reshape(track_count, cam_count, params, capacity, columns...]
    reshape x2 -> x0, local copies, waits for them, and re-layouts: 8.22 us -> none  [the longest x1 4.55 us: on_device(): buffer.reshape(params, columns, track_count, cam_count, capacity)]
    transpose x2 -> x0, local copies, waits for them, and re-layouts: 8.12 us -> none  [the longest x1 5.41 us: on_device(): received = returned.reshape(track_count, cam_count, params, capacity, col...]
  transfers between devices with their start and end apart: 3 -> 4, of which waited for: 3 -> 4; matrix products, arithmetic and copies ran while one was open for 2% -> 1% of each run, Pallas kernels for 0% -> 4%
where the time goes in v1:
time: 136 us; the launch traced here: 134 us
  waiting for transfers between devices  54.2 us (40%)
  starting transfers between devices  44.3 us (33%)
  Pallas kernels  19.6 us (14%)
  blocking collectives  7.72 us (6%)
  local copies, waits for them, and re-layouts  6.68 us (5%)
    all_to_all x3, waiting for transfers between devices, exchange(): parts = lax.all_to_all(parts, axes, split_axis=0, concat_axis=0, tiled=True)  42.5 us
    all_to_all x3, starting transfers between devices, exchange(): parts = lax.all_to_all(parts, axes, split_axis=0, concat_axis=0, tiled=True)  38.9 us
    pallas_call x8, Pallas kernels, call(): pl.pallas_call(kernel, out_shape=tuple((jax.ShapeDtypeStruct(s, d) for s,...  19.6 us
    all_to_all x1, waiting for transfers between devices, on_device(): gram = lax.all_to_all(gram, TRACK, split_axis=0, concat_axis=0, tiled=True)  11.8 us
    all_to_all x1, blocking collectives, on_device(): gram = lax.all_to_all(gram, CAM, split_axis=0, concat_axis=0, tiled=True)  7.72 us
    unnamed x16, local copies, waits for them, and re-layouts  6.6 us
    all_to_all x1, starting transfers between devices, on_device(): gram = lax.all_to_all(gram, TRACK, split_axis=0, concat_axis=0, tiled=True)  5.38 us
  transfers between devices with their start and end apart: 4, of which 4 were waited for; matrix products, arithmetic and copies ran while one was open for 1% of the time, Pallas kernels for 4%

profile of v1, /device:TPU:1, one launch (start us, length us, event | category | flops | bytes accessed | tf_op | source)
XLA Modules:
  0.0 134.4 jit_solution(3082064385517675984)
XLA Ops:
  0.6 0.0 copy-start.2
  0.6 0.8 copy-done.2
  1.4 0.0 copy-start.4
  1.4 0.7 copy-done.4
  2.1 0.0 copy-start.5
  2.1 0.7 copy-done.5
  2.8 1.3 shard_map.94
  4.0 22.2 %all-to-all-start = ((bf16[512,2,128]{2,1,0:T(2,128)(2,1)}), bf16[512,2,128]{2,1,0:T(2,128)(2,1)S(1)}, u32[]{:S(2)}, u32[]{:S(2)}) async-start(bf16[512,2,128]{2,1,0:T(2,128)(2,1)} %bitcast.2), calls=%async_computation | async-start | bytes 524288 | tf_op jit(solution)/shard_map/all_to_all | solution.py:197
  26.2 0.1 pad.3.clone
  26.3 1.1 maximum_maximum_fusion
  27.4 16.2 %all-to-all-done = bf16[512,2,128]{2,1,0:T(2,128)(2,1)S(1)} async-done(((bf16[512,2,128]{2,1,0:T(2,128)(2,1)}), bf16[512,2,128]{2,1,0:T(2,128)(2,1)S(1)}, u32[]{:S(2)}, u32[]{:S(2)}) %all-to-all-start) | async-done | bytes 262176 | tf_op jit(solution)/shard_map/all_to_all | solution.py:197
  43.6 2.5 %shard_map.95 = bf16[1024,128]{1,0:T(8,128)(2,1)} custom-call(bf16[1024,128]{1,0:T(8,128)(2,1)S(1)} %bitcast.21, bf16[1152,128]{1,0:T(8,128)(2,1)S(1)} %bitcast.23), custom_call_target="tpu_custom_call" | custom-call | tf_op jit(solution)/shard_map/pallas_call | solution.py:29
  46.2 8.3 %all-to-all-start.1 = ((bf16[512,2,128]{2,1,0:T(2,128)(2,1)}), bf16[512,2,128]{2,1,0:T(2,128)(2,1)S(1)}, u32[]{:S(2)}, u32[]{:S(2)}) async-start(bf16[512,2,128]{2,1,0:T(2,128)(2,1)} %bitcast.6), calls=%async_computation.1 | async-start | bytes 524288 | tf_op jit(solution)/shard_map/all_to_all | solution.py:197
  54.5 0.0 copy-start.6
  54.5 0.7 copy-done.6
  55.1 0.7 shard_map.96
  55.8 15.9 %all-to-all-done.1 = bf16[512,2,128]{2,1,0:T(2,128)(2,1)S(1)} async-done(((bf16[512,2,128]{2,1,0:T(2,128)(2,1)}), bf16[512,2,128]{2,1,0:T(2,128)(2,1)S(1)}, u32[]{:S(2)}, u32[]{:S(2)}) %all-to-all-start.1) | async-done | bytes 262176 | tf_op jit(solution)/shard_map/all_to_all | solution.py:197
  71.7 0.0 copy-start.3
  71.7 0.7 copy-done.3
  72.4 1.2 shard_map.97
  73.6 8.5 %all-to-all-start.2 = ((bf16[512,2,128]{2,1,0:T(2,128)(2,1)}), bf16[512,2,128]{2,1,0:T(2,128)(2,1)S(1)}, u32[]{:S(2)}, u32[]{:S(2)}) async-start(bf16[512,2,128]{2,1,0:T(2,128)(2,1)} %bitcast.9), calls=%async_computation.2 | async-start | bytes 524288 | tf_op jit(solution)/shard_map/all_to_all | solution.py:197
  82.1 0.0 copy-start
  82.1 0.9 copy-done
  83.0 0.0 copy-start.1
  83.0 0.9 copy-done.1
  83.8 4.9 %shard_map.98 = (bf16[3072,1152]{1,0:T(8,128)(2,1)}, f32[32,1152]{1,0:T(8,128)S(1)}) custom-call(bf16[1024,128]{1,0:T(8,128)(2,1)S(1)} %bitcast.22, bf16[9,32,128]{2,1,0:T(8,128)(2,1)S(1)} %bitcast.27, f32[9,9,128]{2,1,0:T(8,128)S(1)} %copy-done.1), custom_call_target="tpu_custom_call" | custom-call | tf_op jit(solution)/shard_map/pallas_call | solution.py:29
  88.8 10.4 %all-to-all-done.2 = bf16[512,2,128]{2,1,0:T(2,128)(2,1)S(1)} async-done(((bf16[512,2,128]{2,1,0:T(2,128)(2,1)}), bf16[512,2,128]{2,1,0:T(2,128)(2,1)S(1)}, u32[]{:S(2)}, u32[]{:S(2)}) %all-to-all-start.2) | async-done | bytes 262176 | tf_op jit(solution)/shard_map/all_to_all | solution.py:197
  99.1 4.6 %shard_map.99 = (f32[32,1152]{1,0:T(8,128)S(1)}, f32[8,8,128]{2,1,0:T(8,128)S(1)}) custom-call(bf16[1024,128]{1,0:T(8,128)(2,1)S(1)} %bitcast.24, bf16[3072,1152]{1,0:T(8,128)(2,1)} %get-tuple-element.17.weights_ref, f32[32,1152]{1,0:T(8,128)S(1)} %get-tuple-element.18.own_ref), custom_call_target="tpu_custom_call" | custom-call | tf_op jit(solution)/shard_map/pallas_call | solution.py:29
  103.8 7.7 %all_to_all.25.parts_ref = f32[8,8,128]{2,1,0:T(8,128)S(1)} all-to-all(f32[8,8,128]{2,1,0:T(8,128)S(1)} %get-tuple-element.20), channel_id=1, replica_groups=mesh['track_0'=8,'track_1'=8,'cam_0'=4,'cam_1'=2] {'cam_0','cam_1'}, dimensions={0} | all-to-all | bytes 65536 | tf_op jit(solution)/shard_map/all_to_all | solution.py:253
  111.5 0.7 shard_map.100
  112.2 5.4 %all-to-all-start.4 = ((f32[64,8,128]{2,1,0:T(8,128)}), f32[64,8,128]{2,1,0:T(8,128)S(1)}, u32[]{:S(2)}, u32[]{:S(2)}) async-start(f32[64,8,128]{2,1,0:T(8,128)} %shard_map.100), calls=%async_computation.4 | async-start | bytes 524288 | tf_op jit(solution)/shard_map/all_to_all | solution.py:255
  117.6 0.7 copy_bitcast_fusion.1
  118.3 11.8 %all-to-all-done.4.parts_ref = f32[64,8,128]{2,1,0:T(8,128)S(1)} async-done(((f32[64,8,128]{2,1,0:T(8,128)}), f32[64,8,128]{2,1,0:T(8,128)S(1)}, u32[]{:S(2)}, u32[]{:S(2)}) %all-to-all-start.4) | async-done | bytes 262176 | tf_op jit(solution)/shard_map/all_to_all | solution.py:255
  130.0 3.7 %shard_map.101 = (f32[32,1152]{1,0:T(8,128)S(1)}, f32[32,32]{1,0:T(8,128)}) custom-call(f32[64,8,128]{2,1,0:T(8,128)S(1)} %all-to-all-done.4.parts_ref, f32[32,1152]{1,0:T(8,128)S(1)} %get-tuple-element.19.sketch_ref), custom_call_target="tpu_custom_call" | custom-call | tf_op jit(solution)/shard_map/pallas_call | solution.py:29
  133.7 0.7 copy_bitcast_fusion
  (1 shorter events, 0.0 us)
Async XLA Ops:
  0.6 0.8 copy-start.2
  1.4 0.7 copy-start.4
  2.1 0.7 copy-start.5
  4.0 39.6 %all-to-all-start = ((bf16[512,2,128]{2,1,0:T(2,128)(2,1)}), bf16[512,2,128]{2,1,0:T(2,128)(2,1)S(1)}, u32[]{:S(2)}, u32[]{:S(2)}) async-start(bf16[512,2,128]{2,1,0:T(2,128)(2,1)} %bitcast.2), calls=%async_computation | async-start | bytes 524288 | tf_op jit(solution)/shard_map/all_to_all | solution.py:197
  46.2 25.6 %all-to-all-start.1 = ((bf16[512,2,128]{2,1,0:T(2,128)(2,1)}), bf16[512,2,128]{2,1,0:T(2,128)(2,1)S(1)}, u32[]{:S(2)}, u32[]{:S(2)}) async-start(bf16[512,2,128]{2,1,0:T(2,128)(2,1)} %bitcast.6), calls=%async_computation.1 | async-start | bytes 524288 | tf_op jit(solution)/shard_map/all_to_all | solution.py:197
  54.5 0.7 copy-start.6
  71.7 0.7 copy-start.3
  73.6 25.6 %all-to-all-start.2 = ((bf16[512,2,128]{2,1,0:T(2,128)(2,1)}), bf16[512,2,128]{2,1,0:T(2,128)(2,1)S(1)}, u32[]{:S(2)}, u32[]{:S(2)}) async-start(bf16[512,2,128]{2,1,0:T(2,128)(2,1)} %bitcast.9), calls=%async_computation.2 | async-start | bytes 524288 | tf_op jit(solution)/shard_map/all_to_all | solution.py:197
  82.1 0.9 copy-start
  83.0 0.9 copy-start.1
  112.2 17.8 %all-to-all-start.4 = ((f32[64,8,128]{2,1,0:T(8,128)}), f32[64,8,128]{2,1,0:T(8,128)S(1)}, u32[]{:S(2)}, u32[]{:S(2)}) async-start(f32[64,8,128]{2,1,0:T(8,128)} %shard_map.100), calls=%async_computation.4 | async-start | bytes 524288 | tf_op jit(solution)/shard_map/all_to_all | solution.py:255

commit v2 on v1

v2 whole, which is shorter than its diff:
```python
import functools

import jax
import jax.numpy as jnp
from jax import lax
from jax.experimental import pallas as pl
from jax.experimental.pallas import tpu as pltpu
from jax.sharding import Mesh
from jax.sharding import PartitionSpec as P

BLK_OBS = 128
TRK_BLK = 32
LANES = 128
PARAMS = 9
COLS = 32
TRACK = ("track_0", "track_1")
CAM = ("cam_0", "cam_1")
TRACK_CAM = TRACK + CAM
W_ROW = 3 * COLS
ID_ROW = W_ROW + 3 * PARAMS
HIGH = lax.Precision.HIGHEST
F32 = jnp.float32
BF16 = jnp.bfloat16


def dot_lanes(lhs, rhs):
    return lax.dot_general(lhs, rhs, (((1,), (1,)), ((), ())), preferred_element_type=F32)


def call(kernel, shapes, *args, scratch=(), in_specs=None):
    specs = {} if in_specs is None else {"in_specs": in_specs}
    return pl.pallas_call(
        kernel,
        out_shape=tuple(jax.ShapeDtypeStruct(s, d) for s, d in shapes),
        scratch_shapes=list(scratch),
        compiler_params=pltpu.CompilerParams(vmem_limit_bytes=32 << 20),
        **specs,
    )(*args)


def request_kernel(capacity, camera_hbm, mask_hbm, w_hbm, request_ref, slot_ref, camera_ref, mask_ref, w_ref, rows, sems):
    copies = [
        pltpu.make_async_copy(source, target, sems.at[n])
        for n, (source, target) in enumerate(
            ((camera_hbm, camera_ref), (mask_hbm, mask_ref), (w_hbm, w_ref))
        )
    ]
    for copy in copies:
        copy.start()
    rows[...] = jnp.zeros(rows.shape, F32)
    for copy in copies:
        copy.wait()
    obs = camera_ref.shape[1]
    camera = camera_ref[...]
    owner = lax.shift_right_logical(camera, 7)
    owner_f = owner.astype(F32)
    blocks = obs // LANES
    sub = lax.broadcasted_iota(jnp.int32, (LANES, LANES), 0)
    lane = lax.broadcasted_iota(jnp.int32, (LANES, LANES), 1)
    row_of = [owner_f[:, LANES * b : LANES * (b + 1)] for b in range(blocks)]
    column_of = [jnp.broadcast_to(r, (LANES, LANES)).T for r in row_of]
    ranks = []
    for q in range(blocks):
        same = jnp.where((column_of[q] == row_of[q]) & (sub < lane), 1.0, 0.0)
        for b in range(q):
            same = same + jnp.where(column_of[b] == row_of[q], 1.0, 0.0)
        ranks.append(jnp.sum(same, axis=0, keepdims=True))
    slot = owner * capacity + jnp.concatenate(ranks, axis=1).astype(jnp.int32)
    slot_ref[...] = slot
    live = mask_ref[...].astype(F32)
    for m in range(PARAMS):
        rows[W_ROW + 3 * m : W_ROW + 3 * m + 3, :] = w_ref[m].astype(F32) * live
    rows[ID_ROW : ID_ROW + 1, :] = (camera & (LANES - 1)).astype(F32)
    values = rows[...].astype(BF16)
    slots = request_ref.shape[0]
    step = 256
    for s in range(0, slots, step):
        ids = lax.broadcasted_iota(jnp.int32, (step, obs), 0) + s
        chosen = jnp.where(ids == slot, 1.0, 0.0).astype(BF16)
        request_ref[s : s + step, :] = dot_lanes(chosen, values).astype(BF16)


def member_kernel(slot_ref, track_ref, by_track_ref, by_slot_ref):
    obs = slot_ref.shape[1]
    tracks, slots = by_track_ref.shape
    position = lax.broadcasted_iota(jnp.int32, (1, obs), 1)
    track = lax.shift_right_logical(position, 7) * TRK_BLK + track_ref[...]
    ids = lax.broadcasted_iota(jnp.int32, (tracks, obs), 0)
    member = jnp.where(ids == track, 1.0, 0.0).astype(BF16)
    step = 256
    for s in range(0, slots, step):
        ids = lax.broadcasted_iota(jnp.int32, (step, obs), 0) + s
        chosen = jnp.where(ids == slot_ref[...], 1.0, 0.0).astype(BF16)
        by_track_ref[:, s : s + step] = dot_lanes(member, chosen).astype(BF16)
        by_slot_ref[s : s + step, :] = dot_lanes(chosen, member).astype(BF16)


def dot(lhs, rhs):
    return jnp.dot(lhs, rhs, preferred_element_type=F32)


def project_kernel(capacity, request_ref, table_ref, reply_ref, rows, out_rows):
    cams = table_ref.shape[0]
    slots = request_ref.shape[0]
    tracks = slots // (cams * capacity)
    rows[...] = request_ref[...].astype(F32)
    for b in range(cams):
        places = [pl.ds(b * capacity + r, tracks, stride=cams * capacity) for r in range(capacity)]
        turned = jnp.concatenate([rows[p, :] for p in places], axis=0).T
        wanted = lax.broadcasted_iota(jnp.int32, turned.shape, 0).astype(F32)
        chosen = jnp.where(wanted == turned[ID_ROW : ID_ROW + 1, :], 1.0, 0.0).astype(BF16)
        found = dot(table_ref[b], chosen)
        parts = []
        for i in range(3):
            part = jnp.zeros((COLS, turned.shape[1]), F32)
            for m in range(PARAMS):
                w_row = W_ROW + 3 * m + i
                part = part + turned[w_row : w_row + 1, :] * found[COLS * m : COLS * (m + 1), :]
            parts.append(part)
        parts.append(jnp.zeros((LANES - 3 * COLS, turned.shape[1]), F32))
        projected = jnp.concatenate(parts, axis=0).T
        for r, place in enumerate(places):
            out_rows[place, :] = projected[r * tracks : (r + 1) * tracks, :]
    reply_ref[...] = out_rows[...].astype(BF16)


def solve_kernel(reply_ref, by_track_ref, by_slot_ref, v_ref, request_ref, out_ref):
    summed = dot(by_track_ref[...], reply_ref[...]).T
    parts = []
    for i in range(3):
        part = jnp.zeros((COLS, LANES), F32)
        for k in range(3):
            part = part + v_ref[i, k : k + 1, :] * summed[COLS * k : COLS * (k + 1), :]
        parts.append(part)
    parts.append(jnp.zeros((LANES - 3 * COLS, LANES), F32))
    solved = jnp.concatenate(parts, axis=0).astype(BF16)
    spread = dot_lanes(by_slot_ref[...], solved).astype(BF16)
    lane = lax.broadcasted_iota(jnp.int32, spread.shape, 1)
    out_ref[...] = jnp.where(lane < W_ROW, spread, request_ref[...])


def own_kernel(omega_ref, u_ref, own_ref):
    table = [omega_ref[n].astype(F32) for n in range(PARAMS)]
    for m in range(PARAMS):
        total = jnp.zeros(table[0].shape, F32)
        for n in range(PARAMS):
            total = total + u_ref[m, n : n + 1, :] * table[n]
        own_ref[m] = total


def sketch_kernel(solved_ref, own_ref, sketch_ref, gram_ref):
    turned = solved_ref[...].astype(F32).T
    wanted = lax.broadcasted_iota(jnp.int32, turned.shape, 0).astype(F32)
    chosen = jnp.where(wanted == turned[ID_ROW : ID_ROW + 1, :], 1.0, 0.0).astype(BF16)
    tops, rests = [], []
    for m in range(PARAMS):
        part = jnp.zeros((COLS, turned.shape[1]), F32)
        for i in range(3):
            w_row = W_ROW + 3 * m + i
            part = part + turned[w_row : w_row + 1, :] * turned[COLS * i : COLS * (i + 1), :]
        top = part.astype(BF16)
        tops.append(top)
        rests.append((part - top.astype(F32)).astype(BF16))
    summed = dot_lanes(jnp.concatenate(tops + rests, axis=0), chosen)
    half = PARAMS * COLS
    parts = []
    for m in range(PARAMS):
        at = COLS * m
        parts.append(own_ref[m] - (summed[at : at + COLS, :] + summed[half + at : half + at + COLS, :]))
        sketch_ref[m] = parts[m]
    wide = jnp.concatenate(parts, axis=1)
    gram = lax.dot_general(
        wide, wide, (((1,), (1,)), ((), ())), precision=HIGH, preferred_element_type=F32
    )
    packed = jnp.concatenate([gram[8 * q : 8 * q + 8, :] for q in range(4)], axis=1)
    gram_ref[...] = jnp.broadcast_to(packed[None], gram_ref.shape)


def gather_kernel(parts_ref, out_ref):
    out_ref[...] = jnp.broadcast_to(jnp.sum(parts_ref[...], axis=0)[None], out_ref.shape)


def finish_kernel(row_total, parts_ref, sketch_ref, basis_ref, factor_ref):
    packed = jnp.sum(parts_ref[...], axis=0) / row_total
    gram = jnp.concatenate([packed[:, COLS * q : COLS * (q + 1)] for q in range(4)], axis=0)
    row = lax.broadcasted_iota(jnp.int32, (COLS, COLS), 0)
    column = lax.broadcasted_iota(jnp.int32, (COLS, COLS), 1)
    work = jnp.concatenate([gram, jnp.where(row == column, 1.0, 0.0)], axis=1)
    wide_row = lax.broadcasted_iota(jnp.int32, work.shape, 0)
    for k in range(COLS):
        pivot = work[k : k + 1, k : k + 1]
        scale = 1.0 / jnp.sqrt(pivot)
        scaled = work[k : k + 1, :] * scale
        below = work[:, k : k + 1] * scale
        work = jnp.where(
            wide_row > k, work - below * scaled, jnp.where(wide_row == k, scaled, work)
        )
    factor_ref[...] = jnp.where(column >= row, work[:, :COLS], 0.0)
    wide = jnp.concatenate([sketch_ref[m] for m in range(PARAMS)], axis=1)
    basis = jnp.dot(work[:, COLS:], wide, precision=HIGH, preferred_element_type=F32)
    for m in range(PARAMS):
        basis_ref[m] = basis[:, LANES * m : LANES * (m + 1)]


def exchange(values, axes):
    peers = lax.axis_size(axes)
    parts = values.reshape(peers, values.shape[0] // peers, *values.shape[1:])
    parts = lax.all_to_all(parts, axes, split_axis=0, concat_axis=0, tiled=True)
    return parts.reshape(values.shape)


def on_device(omega, u_blocks, w_blocks, v_inverse, obs_camera, obs_track, obs_mask):
    track_count = lax.axis_size(TRACK)
    cam_count = lax.axis_size(CAM)
    devices = track_count * cam_count
    columns, params, cam_width = omega.shape
    obs = obs_camera.shape[0]
    capacity = max(2, 2 * obs // devices)
    slots = devices * capacity
    tracks = obs // BLK_OBS * TRK_BLK
    by_slot_shape = ((slots, LANES), BF16)

    table = omega.transpose(1, 0, 2)
    row_table = lax.all_gather(table.reshape(params * columns, cam_width), CAM)

    request, slot = call(
        functools.partial(request_kernel, capacity),
        (by_slot_shape, ((1, obs), jnp.int32)),
        obs_camera.reshape(1, obs),
        obs_mask.reshape(1, obs),
        w_blocks,
        scratch=(
            pltpu.VMEM((1, obs), jnp.int32),
            pltpu.VMEM((1, obs), jnp.int32),
            pltpu.VMEM(w_blocks.shape, BF16),
            pltpu.VMEM((LANES, obs), F32),
            pltpu.SemaphoreType.DMA((3,)),
        ),
        in_specs=[pl.BlockSpec(memory_space=pl.ANY)] * 3,
    )
    asked = exchange(request, TRACK)
    (reply,) = call(
        functools.partial(project_kernel, capacity),
        (by_slot_shape,),
        asked,
        row_table,
        scratch=(pltpu.VMEM((slots, LANES), F32), pltpu.VMEM((slots, LANES), F32)),
    )
    projected = exchange(reply, TRACK)

    by_track, by_slot = call(
        member_kernel,
        (((tracks, slots), BF16), ((slots, tracks), BF16)),
        slot,
        obs_track.reshape(1, obs),
    )
    (outgoing,) = call(
        solve_kernel, (by_slot_shape,), projected, by_track, by_slot, v_inverse, request
    )
    solved = exchange(outgoing, TRACK_CAM)

    sketch_shape = ((params, columns, cam_width), F32)
    (own,) = call(own_kernel, (sketch_shape,), table, u_blocks)
    sketch, gram = call(
        sketch_kernel, (sketch_shape, ((cam_count, 8, LANES), F32)), solved, own
    )
    gram = lax.all_to_all(gram, CAM, split_axis=0, concat_axis=0, tiled=True)
    (gram,) = call(gather_kernel, (((track_count, 8, LANES), F32),), gram)
    gram = lax.all_to_all(gram, TRACK, split_axis=0, concat_axis=0, tiled=True)
    basis, factor = call(
        functools.partial(finish_kernel, float(params * cam_width * devices)),
        (sketch_shape, ((columns, columns), F32)),
        gram,
        sketch,
    )
    return (sketch.transpose(1, 0, 2), basis.transpose(1, 0, 2), factor)


def solution(mesh):
    track, cam = mesh.devices.shape
    split = Mesh(
        mesh.devices.reshape(8, track // 8, cam // 2, 2), ("track_0", "track_1", "cam_0", "cam_1")
    )
    return jax.shard_map(
        on_device,
        mesh=split,
        in_specs=(
            P(None, None, TRACK_CAM),
            P(None, None, TRACK_CAM),
            P(None, None, TRACK_CAM),
            P(None, None, TRACK_CAM),
            P(TRACK_CAM),
            P(TRACK_CAM),
            P(TRACK_CAM),
        ),
        out_specs=(P(None, None, TRACK_CAM), P(None, None, TRACK_CAM), P()),
        check_vma=False,
    )
```

time: 136 us -> 125 us (0.919)
  blocking collectives: 7.72 us -> 38.9 us
  waiting for transfers between devices: 54.2 us -> 29.4 us
  Pallas kernels: 19.6 us -> 11.1 us
  local copies, waits for them, and re-layouts: 6.68 us -> 2.81 us
  starting transfers between devices: 44.3 us -> 40.5 us
    all_to_all x0 -> x1, blocking collectives: none -> 16.9 us  [on_device(): gram = lax.all_to_all(gram, TRACK, split_axis=0, concat_axis=0, tiled=True)]
    all_gather x0 -> x1, blocking collectives: none -> 14.3 us  [on_device(): row_table = lax.all_gather(table.reshape(params * columns, cam_width), CAM)]
    all_to_all x3, waiting for transfers between devices: 42.5 us -> 29.4 us  [exchange(): parts = lax.all_to_all(parts, axes, split_axis=0, concat_axis=0, tiled=True)]
    all_to_all x1 -> x0, waiting for transfers between devices: 11.8 us -> none  [on_device(): gram = lax.all_to_all(gram, TRACK, split_axis=0, concat_axis=0, tiled=True)]
    pallas_call x8, Pallas kernels: 19.6 us -> 11.1 us  [call(): pl.pallas_call(kernel, out_shape=tuple((jax.ShapeDtypeStruct(s, d) for s,...]
    all_to_all x1 -> x0, starting transfers between devices: 5.38 us -> none  [on_device(): gram = lax.all_to_all(gram, TRACK, split_axis=0, concat_axis=0, tiled=True)]
    unnamed x16, local copies, waits for them, and re-layouts: 6.6 us -> 2.81 us
    all_to_all x3, starting transfers between devices: 38.9 us -> 40.5 us  [exchange(): parts = lax.all_to_all(parts, axes, split_axis=0, concat_axis=0, tiled=True)]
  transfers between devices with their start and end apart: 4 -> 3, of which waited for: 4 -> 2; matrix products, arithmetic and copies ran while one was open for 1% -> 0% of each run, Pallas kernels for 4% -> 1%
where the time goes in v2:
time: 125 us; the launch traced here: 124 us
  starting transfers between devices  40.5 us (32%)
  blocking collectives  38.9 us (31%)
  waiting for transfers between devices  29.4 us (24%)
  Pallas kernels  11.1 us (9%)
  local copies, waits for them, and re-layouts  2.81 us (2%)
    all_to_all x3, starting transfers between devices, exchange(): parts = lax.all_to_all(parts, axes, split_axis=0, concat_axis=0, tiled=True)  40.5 us
    all_to_all x3, waiting for transfers between devices, exchange(): parts = lax.all_to_all(parts, axes, split_axis=0, concat_axis=0, tiled=True)  29.4 us
    all_to_all x1, blocking collectives, on_device(): gram = lax.all_to_all(gram, TRACK, split_axis=0, concat_axis=0, tiled=True)  16.9 us
    all_gather x1, blocking collectives, on_device(): row_table = lax.all_gather(table.reshape(params * columns, cam_width), CAM)  14.3 us
    pallas_call x8, Pallas kernels, call(): pl.pallas_call(kernel, out_shape=tuple((jax.ShapeDtypeStruct(s, d) for s,...  11.1 us
    all_to_all x1, blocking collectives, on_device(): gram = lax.all_to_all(gram, CAM, split_axis=0, concat_axis=0, tiled=True)  7.68 us
    unnamed x16, local copies, waits for them, and re-layouts  2.81 us
  transfers between devices with their start and end apart: 3, of which 2 were waited for; matrix products, arithmetic and copies ran while one was open for 0% of the time, Pallas kernels for 1%

profile of v2, /device:TPU:1, one launch (start us, length us, event | category | flops | bytes accessed | tf_op | source)
XLA Modules:
  0.0 123.5 jit_solution(835409891226770247)
XLA Ops:
  0.6 0.0 copy-start.5
  0.6 0.7 copy-done.5
  1.3 0.0 copy-start.3
  1.3 0.8 copy-done.3
  2.1 0.0 copy-start.6
  2.1 0.7 copy-done.6
  2.8 1.4 %shard_map.94 = (bf16[1024,128]{1,0:T(8,128)(2,1)}, s32[1,512]{1,0:T(1,128)S(1)}) custom-call(s32[1,512]{1,0:T(1,128)S(1)} %bitcast.20, s32[1,512]{1,0:T(1,128)S(1)} %bitcast.21, bf16[9,3,512]{2,1,0:T(4,128)(2,1)S(1)} %copy-done.3), custom_call_target="tpu_custom_call" | custom-call | tf_op jit(solution)/shard_map/pallas_call | solution.py:32
  4.1 0.0 copy-start
  4.2 17.3 %all-to-all-start = ((bf16[64,16,128]{2,1,0:T(8,128)(2,1)}), bf16[64,16,128]{2,1,0:T(8,128)(2,1)S(1)}, u32[]{:S(2)}, u32[]{:S(2)}) async-start(bf16[64,16,128]{2,1,0:T(8,128)(2,1)} %bitcast.2), calls=%async_computation | async-start | bytes 524288 | tf_op jit(solution)/shard_map/all_to_all | solution.py:208
  21.4 0.0 copy-done
  21.4 14.3 %all_gather.3.table_ref = bf16[8,288,128]{2,1,0:T(8,128)(2,1)S(1)} all-gather(bf16[1,288,128]{2,1,0:T(8,128)(2,1)S(1)} %bitcast.17), channel_id=1, replica_groups=mesh['track_0'=8,'track_1'=8,'cam_0'=4,'cam_1'=2] {'cam_0','cam_1'}, dimensions={0}, use_global_device_ids=true | all-gather | bytes 663552 | tf_op jit(solution)/shard_map/all_gather | solution.py:224
  35.8 0.0 all-to-all-done
  35.8 1.4 %shard_map.95 = bf16[1024,128]{1,0:T(8,128)(2,1)} custom-call(bf16[1024,128]{1,0:T(8,128)(2,1)S(1)} %bitcast.15, bf16[8,288,128]{2,1,0:T(8,128)(2,1)S(1)} %all_gather.3.table_ref), custom_call_target="tpu_custom_call" | custom-call | tf_op jit(solution)/shard_map/pallas_call | solution.py:32
  37.2 12.4 %all-to-all-start.1 = ((bf16[64,16,128]{2,1,0:T(8,128)(2,1)}), bf16[64,16,128]{2,1,0:T(8,128)(2,1)S(1)}, u32[]{:S(2)}, u32[]{:S(2)}) async-start(bf16[64,16,128]{2,1,0:T(8,128)(2,1)} %bitcast.6), calls=%async_computation.1 | async-start | bytes 524288 | tf_op jit(solution)/shard_map/all_to_all | solution.py:208
  49.6 0.0 copy-start.7
  49.6 0.0 copy-start.4
  49.6 0.7 copy-done.7
  50.3 0.7 shard_map.96
  50.9 12.0 %all-to-all-done.1 = bf16[64,16,128]{2,1,0:T(8,128)(2,1)S(1)} async-done(((bf16[64,16,128]{2,1,0:T(8,128)(2,1)}), bf16[64,16,128]{2,1,0:T(8,128)(2,1)S(1)}, u32[]{:S(2)}, u32[]{:S(2)}) %all-to-all-start.1) | async-done | bytes 262176 | tf_op jit(solution)/shard_map/all_to_all | solution.py:208
  62.9 0.0 copy-done.4
  62.9 2.1 %shard_map.97 = bf16[1024,128]{1,0:T(8,128)(2,1)} custom-call(bf16[1024,128]{1,0:T(8,128)(2,1)S(1)} %bitcast.14, bf16[128,1024]{1,0:T(8,128)(2,1)S(1)} %get-tuple-element.13.by_track_ref, bf16[1024,128]{1,0:T(8,128)(2,1)S(1)} %get-tuple-element.14.by_slot_ref, f32[3,3,128]{2,1,0:T(4,128)S(1)} %copy-done.4, bf16[1024,128]{1,0:T(8,128)(2,1)} %get-tuple-element.11.request_ref), custom_call_target="tpu_custom_call" | custom-call | tf_op jit(solution)/shard_map/pallas_call | solution.py:32
  65.1 0.0 copy-start.2
  65.1 10.8 %all-to-all-start.2 = ((bf16[512,2,128]{2,1,0:T(2,128)(2,1)}), bf16[512,2,128]{2,1,0:T(2,128)(2,1)S(1)}, u32[]{:S(2)}, u32[]{:S(2)}) async-start(bf16[512,2,128]{2,1,0:T(2,128)(2,1)} %bitcast.9), calls=%async_computation.2 | async-start | bytes 524288 | tf_op jit(solution)/shard_map/all_to_all | solution.py:208
  75.8 0.0 copy-done.2
  75.9 0.1 shard_map.98.own_ref
  76.0 17.5 %all-to-all-done.2 = bf16[512,2,128]{2,1,0:T(2,128)(2,1)S(1)} async-done(((bf16[512,2,128]{2,1,0:T(2,128)(2,1)}), bf16[512,2,128]{2,1,0:T(2,128)(2,1)S(1)}, u32[]{:S(2)}, u32[]{:S(2)}) %all-to-all-start.2) | async-done | bytes 262176 | tf_op jit(solution)/shard_map/all_to_all | solution.py:208
  93.4 1.4 %shard_map.99 = (f32[9,32,128]{2,1,0:T(8,128)}, f32[8,8,128]{2,1,0:T(8,128)S(1)}) custom-call(bf16[1024,128]{1,0:T(8,128)(2,1)S(1)} %bitcast.16, f32[9,32,128]{2,1,0:T(8,128)S(1)} %shard_map.98.own_ref), custom_call_target="tpu_custom_call" | custom-call | tf_op jit(solution)/shard_map/pallas_call | solution.py:32
  94.8 7.7 %all_to_all.25.parts_ref = f32[8,8,128]{2,1,0:T(8,128)S(1)} all-to-all(f32[8,8,128]{2,1,0:T(8,128)S(1)} %get-tuple-element.16), channel_id=1, replica_groups=mesh['track_0'=8,'track_1'=8,'cam_0'=4,'cam_1'=2] {'cam_0','cam_1'}, dimensions={0} | all-to-all | bytes 65536 | tf_op jit(solution)/shard_map/all_to_all | solution.py:267
  102.5 0.0 copy-start.1
  102.5 16.9 %all_to_all.26.parts_ref = f32[64,8,128]{2,1,0:T(8,128)S(1)} all-to-all(f32[64,8,128]{2,1,0:T(8,128)S(1)} %shard_map.100), channel_id=1, replica_groups=mesh['track_0'=8,'track_1'=8,'cam_0'=4,'cam_1'=2] {'track_0','track_1'}, dimensions={0} | all-to-all | bytes 524288 | tf_op jit(solution)/shard_map/all_to_all | solution.py:269
  119.4 0.0 copy-done.1
  119.5 4.1 %shard_map.101 = (f32[9,32,128]{2,1,0:T(8,128)}, f32[32,32]{1,0:T(8,128)}) custom-call(f32[64,8,128]{2,1,0:T(8,128)S(1)} %all_to_all.26.parts_ref, f32[9,32,128]{2,1,0:T(8,128)S(1)} %copy-done.1), custom_call_target="tpu_custom_call" | custom-call | tf_op jit(solution)/shard_map/pallas_call | solution.py:32
  (1 shorter events, 0.0 us)
Async XLA Ops:
  0.6 0.7 copy-start.5
  1.3 0.8 copy-start.3
  2.1 0.7 copy-start.6
  4.1 17.3 %copy-start = (bf16[32,9,128]{2,0,1:T(8,128)(2,1)S(1)}, bf16[32,9,128]{2,0,1:T(8,128)(2,1)}, u32[]{:S(2)}) copy-start(bf16[32,9,128]{2,0,1:T(8,128)(2,1)} %param.7) | copy-start | bytes 221188
  4.2 31.6 %all-to-all-start = ((bf16[64,16,128]{2,1,0:T(8,128)(2,1)}), bf16[64,16,128]{2,1,0:T(8,128)(2,1)S(1)}, u32[]{:S(2)}, u32[]{:S(2)}) async-start(bf16[64,16,128]{2,1,0:T(8,128)(2,1)} %bitcast.2), calls=%async_computation | async-start | bytes 524288 | tf_op jit(solution)/shard_map/all_to_all | solution.py:208
  37.2 25.8 %all-to-all-start.1 = ((bf16[64,16,128]{2,1,0:T(8,128)(2,1)}), bf16[64,16,128]{2,1,0:T(8,128)(2,1)S(1)}, u32[]{:S(2)}, u32[]{:S(2)}) async-start(bf16[64,16,128]{2,1,0:T(8,128)(2,1)} %bitcast.6), calls=%async_computation.1 | async-start | bytes 524288 | tf_op jit(solution)/shard_map/all_to_all | solution.py:208
  49.6 0.7 copy-start.7
  49.6 13.3 %copy-start.4 = (f32[3,3,128]{2,1,0:T(4,128)S(1)}, f32[3,3,128]{2,1,0:T(4,128)}, u32[]{:S(2)}) copy-start(f32[3,3,128]{2,1,0:T(4,128)} %v_ref.1) | copy-start | bytes 13828
  65.1 10.8 %copy-start.2 = (f32[9,9,128]{2,1,0:T(8,128)S(1)}, f32[9,9,128]{2,1,0:T(8,128)}, u32[]{:S(2)}) copy-start(f32[9,9,128]{2,1,0:T(8,128)} %u_ref.1) | copy-start | bytes 124420
  65.1 28.3 %all-to-all-start.2 = ((bf16[512,2,128]{2,1,0:T(2,128)(2,1)}), bf16[512,2,128]{2,1,0:T(2,128)(2,1)S(1)}, u32[]{:S(2)}, u32[]{:S(2)}) async-start(bf16[512,2,128]{2,1,0:T(2,128)(2,1)} %bitcast.9), calls=%async_computation.2 | async-start | bytes 524288 | tf_op jit(solution)/shard_map/all_to_all | solution.py:208
  102.5 16.9 %copy-start.1 = (f32[9,32,128]{2,1,0:T(8,128)S(1)}, f32[9,32,128]{2,1,0:T(8,128)}, u32[]{:S(2)}) copy-start(f32[9,32,128]{2,1,0:T(8,128)} %get-tuple-element.15.sketch_ref) | copy-start | bytes 442372

commit v3 on v2

--- a/solution.py
+++ b/solution.py
@@ -16,6 +16,8 @@
 TRACK = ("track_0", "track_1")
 CAM = ("cam_0", "cam_1")
 TRACK_CAM = TRACK + CAM
+FIRST = ("track_1", "cam_1")
+SECOND = ("track_0", "cam_0")
 W_ROW = 3 * COLS
 ID_ROW = W_ROW + 3 * PARAMS
 HIGH = lax.Precision.HIGHEST
@@ -38,7 +40,20 @@
     )(*args)
 
 
-def request_kernel(capacity, camera_hbm, mask_hbm, w_hbm, request_ref, slot_ref, camera_ref, mask_ref, w_ref, rows, sems):
+def request_kernel(
+    capacity,
+    camera_hbm,
+    mask_hbm,
+    w_hbm,
+    request_ref,
+    slot_ref,
+    values_ref,
+    camera_ref,
+    mask_ref,
+    w_ref,
+    rows,
+    sems,
+):
     copies = [
         pltpu.make_async_copy(source, target, sems.at[n])
         for n, (source, target) in enumerate(
@@ -72,6 +87,7 @@
         rows[W_ROW + 3 * m : W_ROW + 3 * m + 3, :] = w_ref[m].astype(F32) * live
     rows[ID_ROW : ID_ROW + 1, :] = (camera & (LANES - 1)).astype(F32)
     values = rows[...].astype(BF16)
+    values_ref[...] = values
     slots = request_ref.shape[0]
     step = 256
     for s in range(0, slots, step):
@@ -80,7 +96,7 @@
         request_ref[s : s + step, :] = dot_lanes(chosen, values).astype(BF16)
 
 
-def member_kernel(slot_ref, track_ref, by_track_ref, by_slot_ref):
+def member_kernel(slot_ref, track_ref, values_ref, by_track_ref, by_slot_ref, base_ref):
     obs = slot_ref.shape[1]
     tracks, slots = by_track_ref.shape
     position = lax.broadcasted_iota(jnp.int32, (1, obs), 1)
@@ -93,6 +109,7 @@
         chosen = jnp.where(ids == slot_ref[...], 1.0, 0.0).astype(BF16)
         by_track_ref[:, s : s + step] = dot_lanes(member, chosen).astype(BF16)
         by_slot_ref[s : s + step, :] = dot_lanes(chosen, member).astype(BF16)
+        base_ref[s : s + step, :] = dot_lanes(chosen, values_ref[...]).astype(BF16)
 
 
 def dot(lhs, rhs):
@@ -124,7 +141,7 @@
     reply_ref[...] = out_rows[...].astype(BF16)
 
 
-def solve_kernel(reply_ref, by_track_ref, by_slot_ref, v_ref, request_ref, out_ref):
+def solve_kernel(reply_ref, by_track_ref, by_slot_ref, v_ref, base_ref, out_ref):
     summed = dot(by_track_ref[...], reply_ref[...]).T
     parts = []
     for i in range(3):
@@ -136,7 +153,7 @@
     solved = jnp.concatenate(parts, axis=0).astype(BF16)
     spread = dot_lanes(by_slot_ref[...], solved).astype(BF16)
     lane = lax.broadcasted_iota(jnp.int32, spread.shape, 1)
-    out_ref[...] = jnp.where(lane < W_ROW, spread, request_ref[...])
+    out_ref[...] = jnp.where(lane < W_ROW, spread, base_ref[...])
 
 
 def own_kernel(omega_ref, u_ref, own_ref):
@@ -221,14 +238,15 @@
     by_slot_shape = ((slots, LANES), BF16)
 
     table = omega.transpose(1, 0, 2)
-    row_table = lax.all_gather(table.reshape(params * columns, cam_width), CAM)
-
-    request, slot = call(
+    tables = lax.all_gather(table.reshape(params * columns, cam_width), CAM)
+
+    request, slot, values = call(
         functools.partial(request_kernel, capacity),
-        (by_slot_shape, ((1, obs), jnp.int32)),
-        obs_camera.reshape(1, obs),
-        obs_mask.reshape(1, obs),
-        w_blocks,
+        (by_slot_shape, ((1, obs), jnp.int32), ((LANES, obs), BF16)),
+        *(
+            pltpu.with_memory_space_constraint(x, pltpu.HBM)
+            for x in (obs_camera.reshape(1, obs), obs_mask.reshape(1, obs), w_blocks)
+        ),
         scratch=(
             pltpu.VMEM((1, obs), jnp.int32),
             pltpu.VMEM((1, obs), jnp.int32),
@@ -236,37 +254,38 @@
             pltpu.VMEM((LANES, obs), F32),
             pltpu.SemaphoreType.DMA((3,)),
         ),
-        in_specs=[pl.BlockSpec(memory_space=pl.ANY)] * 3,
+        in_specs=[pl.BlockSpec(memory_space=pltpu.HBM)] * 3,
     )
     asked = exchange(request, TRACK)
     (reply,) = call(
         functools.partial(project_kernel, capacity),
         (by_slot_shape,),
         asked,
-        row_table,
+        tables,
         scratch=(pltpu.VMEM((slots, LANES), F32), pltpu.VMEM((slots, LANES), F32)),
     )
     projected = exchange(reply, TRACK)
 
-    by_track, by_slot = call(
+    by_track, by_slot, base = call(
         member_kernel,
-        (((tracks, slots), BF16), ((slots, tracks), BF16)),
+        (((tracks, slots), BF16), ((slots, tracks), BF16), by_slot_shape),
         slot,
         obs_track.reshape(1, obs),
+        values,
     )
     (outgoing,) = call(
-        solve_kernel, (by_slot_shape,), projected, by_track, by_slot, v_inverse, request
+        solve_kernel, (by_slot_shape,), projected, by_track, by_slot, v_inverse, base
     )
     solved = exchange(outgoing, TRACK_CAM)
 
     sketch_shape = ((params, columns, cam_width), F32)
     (own,) = call(own_kernel, (sketch_shape,), table, u_blocks)
     sketch, gram = call(
-        sketch_kernel, (sketch_shape, ((cam_count, 8, LANES), F32)), solved, own
-    )
-    gram = lax.all_to_all(gram, CAM, split_axis=0, concat_axis=0, tiled=True)
-    (gram,) = call(gather_kernel, (((track_count, 8, LANES), F32),), gram)
-    gram = lax.all_to_all(gram, TRACK, split_axis=0, concat_axis=0, tiled=True)
+        sketch_kernel, (sketch_shape, ((lax.axis_size(FIRST), 8, LANES), F32)), solved, own
+    )
+    gram = lax.all_to_all(gram, FIRST, split_axis=0, concat_axis=0, tiled=True)
+    (gram,) = call(gather_kernel, (((lax.axis_size(SECOND), 8, LANES), F32),), gram)
+    gram = lax.all_to_all(gram, SECOND, split_axis=0, concat_axis=0, tiled=True)
     basis, factor = call(
         functools.partial(finish_kernel, float(params * cam_width * devices)),
         (sketch_shape, ((columns, columns), F32)),

time: 125 us -> 122 us (0.976)
  local copies, waits for them, and re-layouts: 2.81 us -> 0.7 us
    unnamed x16 -> x10, local copies, waits for them, and re-layouts: 2.81 us -> 0.7 us
where the time goes in v3:
time: 122 us; the launch traced here: 121 us
  starting transfers between devices  40.5 us (33%)
  blocking collectives  39.2 us (32%)
  waiting for transfers between devices  29.1 us (24%)
  Pallas kernels  11.3 us (9%)
    all_to_all x3, starting transfers between devices, exchange(): parts = lax.all_to_all(parts, axes, split_axis=0, concat_axis=0, tiled=True)  40.5 us
    all_to_all x3, waiting for transfers between devices, exchange(): parts = lax.all_to_all(parts, axes, split_axis=0, concat_axis=0, tiled=True)  29.1 us
    all_gather x1, blocking collectives, on_device(): tables = lax.all_gather(table.reshape(params * columns, cam_width), CAM)  14.3 us
    all_to_all x1, blocking collectives, on_device(): gram = lax.all_to_all(gram, SECOND, split_axis=0, concat_axis=0, tiled=True)  13 us
    all_to_all x1, blocking collectives, on_device(): gram = lax.all_to_all(gram, FIRST, split_axis=0, concat_axis=0, tiled=True)  11.9 us
    pallas_call x8, Pallas kernels, call(): pl.pallas_call(kernel, out_shape=tuple((jax.ShapeDtypeStruct(s, d) for s,...  11.3 us
  transfers between devices with their start and end apart: 3, of which 2 were waited for; matrix products, arithmetic and copies ran while one was open for 0% of the time, Pallas kernels for 1%

profile of v3, /device:TPU:1, one launch (start us, length us, event | category | flops | bytes accessed | tf_op | source)
XLA Modules:
  0.0 121.5 jit_solution(16009732575961076790)
XLA Ops:
  0.6 2.1 %shard_map.94 = (bf16[1024,128]{1,0:T(8,128)(2,1)}, s32[1,512]{1,0:T(1,128)S(1)}, bf16[128,512]{1,0:T(8,128)(2,1)S(1)}) custom-call(s32[1,512]{1,0:T(1,128)} %bitcast.21, s32[1,512]{1,0:T(1,128)} %bitcast.22, bf16[9,3,512]{2,1,0:T(4,128)(2,1)} %w_hbm.1), custom_call_target="tpu_custom_call" | custom-call | tf_op jit(solution)/shard_map/pallas_call | solution.py:34
  2.8 0.0 copy-start
  2.8 17.3 %all-to-all-start = ((bf16[64,16,128]{2,1,0:T(8,128)(2,1)}), bf16[64,16,128]{2,1,0:T(8,128)(2,1)S(1)}, u32[]{:S(2)}, u32[]{:S(2)}) async-start(bf16[64,16,128]{2,1,0:T(8,128)(2,1)} %bitcast.2), calls=%async_computation | async-start | bytes 524288 | tf_op jit(solution)/shard_map/all_to_all | solution.py:225
  20.1 0.0 copy-done
  20.1 14.3 %all_gather.3.table_ref = bf16[8,288,128]{2,1,0:T(8,128)(2,1)S(1)} all-gather(bf16[1,288,128]{2,1,0:T(8,128)(2,1)S(1)} %bitcast.17), channel_id=1, replica_groups=mesh['track_0'=8,'track_1'=8,'cam_0'=4,'cam_1'=2] {'cam_0','cam_1'}, dimensions={0}, use_global_device_ids=true | all-gather | bytes 663552 | tf_op jit(solution)/shard_map/all_gather | solution.py:241
  34.4 0.0 all-to-all-done
  34.4 1.4 %shard_map.95 = bf16[1024,128]{1,0:T(8,128)(2,1)} custom-call(bf16[1024,128]{1,0:T(8,128)(2,1)S(1)} %bitcast.15, bf16[8,288,128]{2,1,0:T(8,128)(2,1)S(1)} %all_gather.3.table_ref), custom_call_target="tpu_custom_call" | custom-call | tf_op jit(solution)/shard_map/pallas_call | solution.py:34
  35.8 12.4 %all-to-all-start.1 = ((bf16[64,16,128]{2,1,0:T(8,128)(2,1)}), bf16[64,16,128]{2,1,0:T(8,128)(2,1)S(1)}, u32[]{:S(2)}, u32[]{:S(2)}) async-start(bf16[64,16,128]{2,1,0:T(8,128)(2,1)} %bitcast.6), calls=%async_computation.1 | async-start | bytes 524288 | tf_op jit(solution)/shard_map/all_to_all | solution.py:225
  48.3 0.0 copy-start.4
  48.3 0.7 copy-done.4
  49.0 0.9 shard_map.96
  49.9 0.0 copy-start.3
  49.9 11.7 %all-to-all-done.1 = bf16[64,16,128]{2,1,0:T(8,128)(2,1)S(1)} async-done(((bf16[64,16,128]{2,1,0:T(8,128)(2,1)}), bf16[64,16,128]{2,1,0:T(8,128)(2,1)S(1)}, u32[]{:S(2)}, u32[]{:S(2)}) %all-to-all-start.1) | async-done | bytes 262176 | tf_op jit(solution)/shard_map/all_to_all | solution.py:225
  61.6 0.0 copy-done.3
  61.6 1.2 shard_map.97
  62.8 0.0 copy-start.2
  62.8 10.8 %all-to-all-start.2 = ((bf16[512,2,128]{2,1,0:T(2,128)(2,1)}), bf16[512,2,128]{2,1,0:T(2,128)(2,1)S(1)}, u32[]{:S(2)}, u32[]{:S(2)}) async-start(bf16[512,2,128]{2,1,0:T(2,128)(2,1)} %bitcast.9), calls=%async_computation.2 | async-start | bytes 524288 | tf_op jit(solution)/shard_map/all_to_all | solution.py:225
  73.6 0.0 copy-done.2
  73.6 0.1 shard_map.98.own_ref
  73.7 17.4 %all-to-all-done.2 = bf16[512,2,128]{2,1,0:T(2,128)(2,1)S(1)} async-done(((bf16[512,2,128]{2,1,0:T(2,128)(2,1)}), bf16[512,2,128]{2,1,0:T(2,128)(2,1)S(1)}, u32[]{:S(2)}, u32[]{:S(2)}) %all-to-all-start.2) | async-done | bytes 262176 | tf_op jit(solution)/shard_map/all_to_all | solution.py:225
  91.1 1.4 %shard_map.99 = (f32[9,32,128]{2,1,0:T(8,128)}, f32[16,8,128]{2,1,0:T(8,128)S(1)}) custom-call(bf16[1024,128]{1,0:T(8,128)(2,1)S(1)} %bitcast.16, f32[9,32,128]{2,1,0:T(8,128)S(1)} %shard_map.98.own_ref), custom_call_target="tpu_custom_call" | custom-call | tf_op jit(solution)/shard_map/pallas_call | solution.py:34
  92.5 11.9 %all_to_all.25.parts_ref = f32[16,8,128]{2,1,0:T(8,128)S(1)} all-to-all(f32[16,8,128]{2,1,0:T(8,128)S(1)} %get-tuple-element.20), channel_id=1, replica_groups=mesh['track_0'=8,'track_1'=8,'cam_0'=4,'cam_1'=2] {'track_1','cam_1'}, dimensions={0} | all-to-all | bytes 131072 | tf_op jit(solution)/shard_map/all_to_all | solution.py:286
  104.4 0.0 copy-start.1
  104.4 13.0 %all_to_all.26.parts_ref = f32[32,8,128]{2,1,0:T(8,128)S(1)} all-to-all(f32[32,8,128]{2,1,0:T(8,128)S(1)} %shard_map.100), channel_id=1, replica_groups=mesh['track_0'=8,'track_1'=8,'cam_0'=4,'cam_1'=2] {'track_0','cam_0'}, dimensions={0} | all-to-all | bytes 262144 | tf_op jit(solution)/shard_map/all_to_all | solution.py:288
  117.4 0.0 copy-done.1
  117.4 4.1 %shard_map.101 = (f32[9,32,128]{2,1,0:T(8,128)}, f32[32,32]{1,0:T(8,128)}) custom-call(f32[32,8,128]{2,1,0:T(8,128)S(1)} %all_to_all.26.parts_ref, f32[9,32,128]{2,1,0:T(8,128)S(1)} %copy-done.1), custom_call_target="tpu_custom_call" | custom-call | tf_op jit(solution)/shard_map/pallas_call | solution.py:34
  (1 shorter events, 0.0 us)
Async XLA Ops:
  2.8 17.3 %copy-start = (bf16[32,9,128]{2,0,1:T(8,128)(2,1)S(1)}, bf16[32,9,128]{2,0,1:T(8,128)(2,1)}, u32[]{:S(2)}) copy-start(bf16[32,9,128]{2,0,1:T(8,128)(2,1)} %param.7) | copy-start | bytes 221188
  2.8 31.6 %all-to-all-start = ((bf16[64,16,128]{2,1,0:T(8,128)(2,1)}), bf16[64,16,128]{2,1,0:T(8,128)(2,1)S(1)}, u32[]{:S(2)}, u32[]{:S(2)}) async-start(bf16[64,16,128]{2,1,0:T(8,128)(2,1)} %bitcast.2), calls=%async_computation | async-start | bytes 524288 | tf_op jit(solution)/shard_map/all_to_all | solution.py:225
  35.8 25.8 %all-to-all-start.1 = ((bf16[64,16,128]{2,1,0:T(8,128)(2,1)}), bf16[64,16,128]{2,1,0:T(8,128)(2,1)S(1)}, u32[]{:S(2)}, u32[]{:S(2)}) async-start(bf16[64,16,128]{2,1,0:T(8,128)(2,1)} %bitcast.6), calls=%async_computation.1 | async-start | bytes 524288 | tf_op jit(solution)/shard_map/all_to_all | solution.py:225
  48.3 0.7 copy-start.4
  49.9 11.7 %copy-start.3 = (f32[3,3,128]{2,1,0:T(4,128)S(1)}, f32[3,3,128]{2,1,0:T(4,128)}, u32[]{:S(2)}) copy-start(f32[3,3,128]{2,1,0:T(4,128)} %v_ref.1) | copy-start | bytes 13828
  62.8 10.8 %copy-start.2 = (f32[9,9,128]{2,1,0:T(8,128)S(1)}, f32[9,9,128]{2,1,0:T(8,128)}, u32[]{:S(2)}) copy-start(f32[9,9,128]{2,1,0:T(8,128)} %u_ref.1) | copy-start | bytes 124420
  62.8 28.3 %all-to-all-start.2 = ((bf16[512,2,128]{2,1,0:T(2,128)(2,1)}), bf16[512,2,128]{2,1,0:T(2,128)(2,1)S(1)}, u32[]{:S(2)}, u32[]{:S(2)}) async-start(bf16[512,2,128]{2,1,0:T(2,128)(2,1)} %bitcast.9), calls=%async_computation.2 | async-start | bytes 524288 | tf_op jit(solution)/shard_map/all_to_all | solution.py:225
  104.4 13.0 %copy-start.1 = (f32[9,32,128]{2,1,0:T(8,128)S(1)}, f32[9,32,128]{2,1,0:T(8,128)}, u32[]{:S(2)}) copy-start(f32[9,32,128]{2,1,0:T(8,128)} %get-tuple-element.19.sketch_ref) | copy-start | bytes 442372

commit v4 on v3

--- a/solution.py
+++ b/solution.py
@@ -41,7 +41,7 @@
 
 
 def request_kernel(
-    capacity,
+    sizes,
     camera_hbm,
     mask_hbm,
     w_hbm,
@@ -54,6 +54,7 @@
     rows,
     sems,
 ):
+    capacity, head, block = sizes
     copies = [
         pltpu.make_async_copy(source, target, sems.at[n])
         for n, (source, target) in enumerate(
@@ -82,6 +83,8 @@
         ranks.append(jnp.sum(same, axis=0, keepdims=True))
     slot = owner * capacity + jnp.concatenate(ranks, axis=1).astype(jnp.int32)
     slot_ref[...] = slot
+    at_head = (slot >= head) & (slot < head + block)
+    slot = jnp.where(slot < block, slot + head, jnp.where(at_head, slot - head, slot))
     live = mask_ref[...].astype(F32)
     for m in range(PARAMS):
         rows[W_ROW + 3 * m : W_ROW + 3 * m + 3, :] = w_ref[m].astype(F32) * live
@@ -116,7 +119,8 @@
     return jnp.dot(lhs, rhs, preferred_element_type=F32)
 
 
-def project_kernel(capacity, request_ref, table_ref, reply_ref, rows, out_rows):
+def project_kernel(sizes, request_ref, table_ref, reply_ref, rows, out_rows):
+    capacity, head, block = sizes
     cams = table_ref.shape[0]
     slots = request_ref.shape[0]
     tracks = slots // (cams * capacity)
@@ -139,6 +143,8 @@
         for r, place in enumerate(places):
             out_rows[place, :] = projected[r * tracks : (r + 1) * tracks, :]
     reply_ref[...] = out_rows[...].astype(BF16)
+    reply_ref[0:block, :] = out_rows[head : head + block, :].astype(BF16)
+    reply_ref[head : head + block, :] = out_rows[0:block, :].astype(BF16)
 
 
 def solve_kernel(reply_ref, by_track_ref, by_slot_ref, v_ref, base_ref, out_ref):
@@ -204,14 +210,14 @@
     column = lax.broadcasted_iota(jnp.int32, (COLS, COLS), 1)
     work = jnp.concatenate([gram, jnp.where(row == column, 1.0, 0.0)], axis=1)
     wide_row = lax.broadcasted_iota(jnp.int32, work.shape, 0)
-    for k in range(COLS):
-        pivot = work[k : k + 1, k : k + 1]
-        scale = 1.0 / jnp.sqrt(pivot)
-        scaled = work[k : k + 1, :] * scale
-        below = work[:, k : k + 1] * scale
-        work = jnp.where(
-            wide_row > k, work - below * scaled, jnp.where(wide_row == k, scaled, work)
-        )
+    pivots = jnp.broadcast_to(work[:, 0:1], work.shape)
+    for k in range(COLS - 1):
+        ahead = jnp.broadcast_to(work[:, k + 1 : k + 2], work.shape)
+        below = jnp.where(wide_row > k, pivots, 0.0) * (1.0 / pivots[k : k + 1, :])
+        pivots = ahead - below * pivots[k + 1 : k + 2, :]
+        work = work - below * work[k : k + 1, :]
+    diagonal = jnp.sum(jnp.where(row == column, work[:, :COLS], 0.0), axis=1, keepdims=True)
+    work = work * (1.0 / jnp.sqrt(diagonal))
     factor_ref[...] = jnp.where(column >= row, work[:, :COLS], 0.0)
     wide = jnp.concatenate([sketch_ref[m] for m in range(PARAMS)], axis=1)
     basis = jnp.dot(work[:, COLS:], wide, precision=HIGH, preferred_element_type=F32)
@@ -219,10 +225,27 @@
         basis_ref[m] = basis[:, LANES * m : LANES * (m + 1)]
 
 
-def exchange(values, axes):
+def middle(axes):
+    index = 0
+    for axis in axes:
+        size = lax.axis_size(axis)
+        index = index * size + (size // 2 if size > 2 else 0)
+    return index
+
+
+def exchange(values, axes, first=0):
     peers = lax.axis_size(axes)
     parts = values.reshape(peers, values.shape[0] // peers, *values.shape[1:])
-    parts = lax.all_to_all(parts, axes, split_axis=0, concat_axis=0, tiled=True)
+    order = list(range(peers))
+    order[0], order[first] = first, 0
+    parts = lax.all_to_all(
+        parts,
+        axes,
+        split_axis=0,
+        concat_axis=0,
+        tiled=True,
+        axis_index_groups=[order] if first else None,
+    )
     return parts.reshape(values.shape)
 
 
@@ -240,8 +263,10 @@
     table = omega.transpose(1, 0, 2)
     tables = lax.all_gather(table.reshape(params * columns, cam_width), CAM)
 
+    head = middle(TRACK)
+    block = cam_count * capacity
     request, slot, values = call(
-        functools.partial(request_kernel, capacity),
+        functools.partial(request_kernel, (capacity, head * block, block)),
         (by_slot_shape, ((1, obs), jnp.int32), ((LANES, obs), BF16)),
         *(
             pltpu.with_memory_space_constraint(x, pltpu.HBM)
@@ -256,9 +281,9 @@
         ),
         in_specs=[pl.BlockSpec(memory_space=pltpu.HBM)] * 3,
     )
-    asked = exchange(request, TRACK)
+    asked = exchange(request, TRACK, head)
     (reply,) = call(
-        functools.partial(project_kernel, capacity),
+        functools.partial(project_kernel, (capacity, head * block, block)),
         (by_slot_shape,),
         asked,
         tables,
@@ -283,9 +308,9 @@
     sketch, gram = call(
         sketch_kernel, (sketch_shape, ((lax.axis_size(FIRST), 8, LANES), F32)), solved, own
     )
-    gram = lax.all_to_all(gram, FIRST, split_axis=0, concat_axis=0, tiled=True)
+    gram = exchange(gram, FIRST, middle(FIRST))
     (gram,) = call(gather_kernel, (((lax.axis_size(SECOND), 8, LANES), F32),), gram)
-    gram = lax.all_to_all(gram, SECOND, split_axis=0, concat_axis=0, tiled=True)
+    gram = exchange(gram, SECOND, middle(SECOND))
     basis, factor = call(
         functools.partial(finish_kernel, float(params * cam_width * devices)),
         (sketch_shape, ((columns, columns), F32)),

time: 122 us -> 113 us (0.926)
  starting transfers between devices: 40.5 us -> 35.1 us
  blocking collectives: 39.2 us -> 37.3 us
  Pallas kernels: 11.3 us -> 9.68 us
    all_to_all x3, starting transfers between devices: 40.5 us -> 35.1 us  [exchange(): lax.all_to_all(parts, axes, split_axis=0, concat_axis=0, tiled=True, axis...]
    all_to_all x2, blocking collectives: 24.9 us -> 22.7 us  [exchange(): lax.all_to_all(parts, axes, split_axis=0, concat_axis=0, tiled=True, axis...]
    pallas_call x8, Pallas kernels: 11.3 us -> 9.68 us  [call(): pl.pallas_call(kernel, out_shape=tuple((jax.ShapeDtypeStruct(s, d) for s,...]
where the time goes in v4:
time: 113 us
  blocking collectives  37.3 us (33%)
  starting transfers between devices  35.1 us (31%)
  waiting for transfers between devices  29.4 us (26%)
  Pallas kernels  9.68 us (9%)
    all_to_all x3, starting transfers between devices, exchange(): lax.all_to_all(parts, axes, split_axis=0, concat_axis=0, tiled=True, axis...  35.1 us
    all_to_all x3, waiting for transfers between devices, exchange(): lax.all_to_all(parts, axes, split_axis=0, concat_axis=0, tiled=True, axis...  29.4 us
    all_to_all x2, blocking collectives, exchange(): lax.all_to_all(parts, axes, split_axis=0, concat_axis=0, tiled=True, axis...  22.7 us
    all_gather x1, blocking collectives, on_device(): tables = lax.all_gather(table.reshape(params * columns, cam_width), CAM)  14.6 us
    pallas_call x8, Pallas kernels, call(): pl.pallas_call(kernel, out_shape=tuple((jax.ShapeDtypeStruct(s, d) for s,...  9.68 us
  transfers between devices with their start and end apart: 3, of which 2 were waited for; matrix products, arithmetic and copies ran while one was open for 0% of the time, Pallas kernels for 1%

profile of v4, /device:TPU:1, one launch (start us, length us, event | category | flops | bytes accessed | tf_op | source)
XLA Modules:
  0.0 112.9 jit_solution(596137413515530344)
XLA Ops:
  0.6 2.1 %shard_map.94 = (bf16[1024,128]{1,0:T(8,128)(2,1)}, s32[1,512]{1,0:T(1,128)S(1)}, bf16[128,512]{1,0:T(8,128)(2,1)S(1)}) custom-call(s32[1,512]{1,0:T(1,128)} %bitcast.33, s32[1,512]{1,0:T(1,128)} %bitcast.34, bf16[9,3,512]{2,1,0:T(4,128)(2,1)} %w_hbm.1), custom_call_target="tpu_custom_call" | custom-call | tf_op jit(solution)/shard_map/pallas_call | solution.py:34
  2.8 0.0 copy-start
  2.8 20.3 %all-to-all-start = ((bf16[64,16,128]{2,1,0:T(8,128)(2,1)}), bf16[64,16,128]{2,1,0:T(8,128)(2,1)S(1)}, u32[]{:S(2)}, u32[]{:S(2)}) async-start(bf16[64,16,128]{2,1,0:T(8,128)(2,1)} %bitcast.2), calls=%async_computation | async-start | bytes 524288 | tf_op jit(solution)/shard_map/all_to_all | solution.py:241
  23.1 0.0 copy-done
  23.1 14.6 %all_gather.3.table_ref = bf16[8,288,128]{2,1,0:T(8,128)(2,1)S(1)} all-gather(bf16[1,288,128]{2,1,0:T(8,128)(2,1)S(1)} %bitcast.27), channel_id=1, replica_groups=mesh['track_0'=8,'track_1'=8,'cam_0'=4,'cam_1'=2] {'cam_0','cam_1'}, dimensions={0}, use_global_device_ids=true | all-gather | bytes 663552 | tf_op jit(solution)/shard_map/all_gather | solution.py:264
  37.7 0.0 all-to-all-done
  37.7 1.4 %shard_map.95 = bf16[1024,128]{1,0:T(8,128)(2,1)} custom-call(bf16[1024,128]{1,0:T(8,128)(2,1)S(1)} %bitcast.23, bf16[8,288,128]{2,1,0:T(8,128)(2,1)S(1)} %all_gather.3.table_ref), custom_call_target="tpu_custom_call" | custom-call | tf_op jit(solution)/shard_map/pallas_call | solution.py:34
  39.1 4.6 %all-to-all-start.1 = ((bf16[64,16,128]{2,1,0:T(8,128)(2,1)}), bf16[64,16,128]{2,1,0:T(8,128)(2,1)S(1)}, u32[]{:S(2)}, u32[]{:S(2)}) async-start(bf16[64,16,128]{2,1,0:T(8,128)(2,1)} %bitcast.6), calls=%async_computation.1 | async-start | bytes 524288 | tf_op jit(solution)/shard_map/all_to_all | solution.py:241
  43.7 0.0 copy-start.4
  43.7 0.7 copy-done.4
  44.4 0.9 shard_map.96
  45.4 0.0 copy-start.3
  45.4 12.0 %all-to-all-done.1 = bf16[64,16,128]{2,1,0:T(8,128)(2,1)S(1)} async-done(((bf16[64,16,128]{2,1,0:T(8,128)(2,1)}), bf16[64,16,128]{2,1,0:T(8,128)(2,1)S(1)}, u32[]{:S(2)}, u32[]{:S(2)}) %all-to-all-start.1) | async-done | bytes 262176 | tf_op jit(solution)/shard_map/all_to_all | solution.py:241
  57.3 0.0 copy-done.3
  57.3 1.2 %shard_map.97 = bf16[1024,128]{1,0:T(8,128)(2,1)} custom-call(bf16[1024,128]{1,0:T(8,128)(2,1)S(1)} %bitcast.22, bf16[128,1024]{1,0:T(8,128)(2,1)S(1)} %get-tuple-element.16.by_track_ref, bf16[1024,128]{1,0:T(8,128)(2,1)S(1)} %get-tuple-element.17.by_slot_ref, f32[3,3,128]{2,1,0:T(4,128)S(1)} %copy-done.3, bf16[1024,128]{1,0:T(8,128)(2,1)S(1)} %get-tuple-element.18.base_ref), custom_call_target="tpu_custom_call" | custom-call | tf_op jit(solution)/shard_map/pallas_call | solution.py:34
  58.5 0.0 copy-start.2
  58.5 10.2 %all-to-all-start.2 = ((bf16[512,2,128]{2,1,0:T(2,128)(2,1)}), bf16[512,2,128]{2,1,0:T(2,128)(2,1)S(1)}, u32[]{:S(2)}, u32[]{:S(2)}) async-start(bf16[512,2,128]{2,1,0:T(2,128)(2,1)} %bitcast.9), calls=%async_computation.2 | async-start | bytes 524288 | tf_op jit(solution)/shard_map/all_to_all | solution.py:241
  68.8 0.0 copy-done.2
  68.8 0.1 shard_map.98.own_ref
  68.9 17.4 %all-to-all-done.2 = bf16[512,2,128]{2,1,0:T(2,128)(2,1)S(1)} async-done(((bf16[512,2,128]{2,1,0:T(2,128)(2,1)}), bf16[512,2,128]{2,1,0:T(2,128)(2,1)S(1)}, u32[]{:S(2)}, u32[]{:S(2)}) %all-to-all-start.2) | async-done | bytes 262176 | tf_op jit(solution)/shard_map/all_to_all | solution.py:241
  86.3 1.4 %shard_map.99 = (f32[9,32,128]{2,1,0:T(8,128)}, f32[16,8,128]{2,1,0:T(8,128)S(1)}) custom-call(bf16[1024,128]{1,0:T(8,128)(2,1)S(1)} %bitcast.24, f32[9,32,128]{2,1,0:T(8,128)S(1)} %shard_map.98.own_ref), custom_call_target="tpu_custom_call" | custom-call | tf_op jit(solution)/shard_map/pallas_call | solution.py:34
  87.7 9.6 %all_to_all.25 = f32[16,1,8,128]{3,2,1,0:T(8,128)S(1)} all-to-all(f32[16,1,8,128]{3,2,1,0:T(8,128)S(1)} %bitcast.31), channel_id=1, replica_groups={{32,1,8,9,16,17,24,25,0,33,40,41,48,49,56,57},{34,3,10,11,18,19,26,27,2..., dimensions={0} | all-to-all | bytes 131072 | tf_op jit(solution)/shard_map/all_to_all | solution.py:241
  97.3 0.0 copy-start.1
  97.3 13.1 %all_to_all.26 = f32[32,1,8,128]{3,2,1,0:T(8,128)S(1)} all-to-all(f32[32,1,8,128]{3,2,1,0:T(8,128)S(1)} %bitcast.26), channel_id=1, replica_groups={{260,2,4,6,64,66,68,70,128,130,132,134,192,194,196,198,256,258,0,262,32..., dimensions={0} | all-to-all | bytes 262144 | tf_op jit(solution)/shard_map/all_to_all | solution.py:241
  110.4 0.0 copy-done.1
  110.4 2.5 %shard_map.101 = (f32[9,32,128]{2,1,0:T(8,128)}, f32[32,32]{1,0:T(8,128)}) custom-call(f32[32,8,128]{2,1,0:T(8,128)S(1)} %bitcast.25, f32[9,32,128]{2,1,0:T(8,128)S(1)} %copy-done.1), custom_call_target="tpu_custom_call" | custom-call | tf_op jit(solution)/shard_map/pallas_call | solution.py:34
  (1 shorter events, 0.0 us)
Async XLA Ops:
  2.8 20.3 %copy-start = (bf16[32,9,128]{2,0,1:T(8,128)(2,1)S(1)}, bf16[32,9,128]{2,0,1:T(8,128)(2,1)}, u32[]{:S(2)}) copy-start(bf16[32,9,128]{2,0,1:T(8,128)(2,1)} %param.7) | copy-start | bytes 221188
  2.8 34.9 %all-to-all-start = ((bf16[64,16,128]{2,1,0:T(8,128)(2,1)}), bf16[64,16,128]{2,1,0:T(8,128)(2,1)S(1)}, u32[]{:S(2)}, u32[]{:S(2)}) async-start(bf16[64,16,128]{2,1,0:T(8,128)(2,1)} %bitcast.2), calls=%async_computation | async-start | bytes 524288 | tf_op jit(solution)/shard_map/all_to_all | solution.py:241
  39.1 18.2 %all-to-all-start.1 = ((bf16[64,16,128]{2,1,0:T(8,128)(2,1)}), bf16[64,16,128]{2,1,0:T(8,128)(2,1)S(1)}, u32[]{:S(2)}, u32[]{:S(2)}) async-start(bf16[64,16,128]{2,1,0:T(8,128)(2,1)} %bitcast.6), calls=%async_computation.1 | async-start | bytes 524288 | tf_op jit(solution)/shard_map/all_to_all | solution.py:241
  43.7 0.7 copy-start.4
  45.4 12.0 %copy-start.3 = (f32[3,3,128]{2,1,0:T(4,128)S(1)}, f32[3,3,128]{2,1,0:T(4,128)}, u32[]{:S(2)}) copy-start(f32[3,3,128]{2,1,0:T(4,128)} %v_ref.1) | copy-start | bytes 13828
  58.5 10.2 %copy-start.2 = (f32[9,9,128]{2,1,0:T(8,128)S(1)}, f32[9,9,128]{2,1,0:T(8,128)}, u32[]{:S(2)}) copy-start(f32[9,9,128]{2,1,0:T(8,128)} %u_ref.1) | copy-start | bytes 124420
  58.5 27.8 %all-to-all-start.2 = ((bf16[512,2,128]{2,1,0:T(2,128)(2,1)}), bf16[512,2,128]{2,1,0:T(2,128)(2,1)S(1)}, u32[]{:S(2)}, u32[]{:S(2)}) async-start(bf16[512,2,128]{2,1,0:T(2,128)(2,1)} %bitcast.9), calls=%async_computation.2 | async-start | bytes 524288 | tf_op jit(solution)/shard_map/all_to_all | solution.py:241
  97.3 13.1 %copy-start.1 = (f32[9,32,128]{2,1,0:T(8,128)S(1)}, f32[9,32,128]{2,1,0:T(8,128)}, u32[]{:S(2)}) copy-start(f32[9,32,128]{2,1,0:T(8,128)} %get-tuple-element.19.sketch_ref) | copy-start | bytes 442372

commit v5 on v4

--- a/solution.py
+++ b/solution.py
@@ -162,16 +162,17 @@
     out_ref[...] = jnp.where(lane < W_ROW, spread, base_ref[...])
 
 
-def own_kernel(omega_ref, u_ref, own_ref):
+def own_term(omega_ref, u_ref):
     table = [omega_ref[n].astype(F32) for n in range(PARAMS)]
     for m in range(PARAMS):
         total = jnp.zeros(table[0].shape, F32)
         for n in range(PARAMS):
             total = total + u_ref[m, n : n + 1, :] * table[n]
-        own_ref[m] = total
-
-
-def sketch_kernel(solved_ref, own_ref, sketch_ref, gram_ref):
+        yield total
+
+
+def sketch_kernel(solved_ref, omega_ref, u_ref, sketch_ref, gram_ref):
+    own = list(own_term(omega_ref, u_ref))
     turned = solved_ref[...].astype(F32).T
     wanted = lax.broadcasted_iota(jnp.int32, turned.shape, 0).astype(F32)
     chosen = jnp.where(wanted == turned[ID_ROW : ID_ROW + 1, :], 1.0, 0.0).astype(BF16)
@@ -189,7 +190,7 @@
     parts = []
     for m in range(PARAMS):
         at = COLS * m
-        parts.append(own_ref[m] - (summed[at : at + COLS, :] + summed[half + at : half + at + COLS, :]))
+        parts.append(own[m] - (summed[at : at + COLS, :] + summed[half + at : half + at + COLS, :]))
         sketch_ref[m] = parts[m]
     wide = jnp.concatenate(parts, axis=1)
     gram = lax.dot_general(
@@ -304,9 +305,12 @@
     solved = exchange(outgoing, TRACK_CAM)
 
     sketch_shape = ((params, columns, cam_width), F32)
-    (own,) = call(own_kernel, (sketch_shape,), table, u_blocks)
     sketch, gram = call(
-        sketch_kernel, (sketch_shape, ((lax.axis_size(FIRST), 8, LANES), F32)), solved, own
+        sketch_kernel,
+        (sketch_shape, ((lax.axis_size(FIRST), 8, LANES), F32)),
+        solved,
+        table,
+        u_blocks,
     )
     gram = exchange(gram, FIRST, middle(FIRST))
     (gram,) = call(gather_kernel, (((lax.axis_size(SECOND), 8, LANES), F32),), gram)

time: 113 us -> 113 us (level)
  blocking collectives: 37.3 us -> 65.4 us
  waiting for transfers between devices: 29.4 us -> 12 us
  starting transfers between devices: 35.1 us -> 24.9 us
    all_to_all x2 -> x3, blocking collectives: 22.7 us -> 50.8 us  [exchange(): lax.all_to_all(parts, axes, split_axis=0, concat_axis=0, tiled=True, axis...]
    all_to_all x3 -> x2, waiting for transfers between devices: 29.4 us -> 12 us  [exchange(): lax.all_to_all(parts, axes, split_axis=0, concat_axis=0, tiled=True, axis...]
    all_to_all x3 -> x2, starting transfers between devices: 35.1 us -> 24.9 us  [exchange(): lax.all_to_all(parts, axes, split_axis=0, concat_axis=0, tiled=True, axis...]
    pallas_call x8 -> x7, Pallas kernels: 9.68 us -> 8.88 us  [call(): pl.pallas_call(kernel, out_shape=tuple((jax.ShapeDtypeStruct(s, d) for s,...]
  transfers between devices with their start and end apart: 3 -> 2, of which waited for: 2 -> 1; matrix products, arithmetic and copies ran while one was open for 0% -> 0% of each run, Pallas kernels for 1% -> 1%
where the time goes in v5:
time: 113 us
  blocking collectives  65.4 us (58%)
  starting transfers between devices  24.9 us (22%)
  waiting for transfers between devices  12 us (11%)
  Pallas kernels  8.88 us (8%)
    all_to_all x3, blocking collectives, exchange(): lax.all_to_all(parts, axes, split_axis=0, concat_axis=0, tiled=True, axis...  50.8 us
    all_to_all x2, starting transfers between devices, exchange(): lax.all_to_all(parts, axes, split_axis=0, concat_axis=0, tiled=True, axis...  24.9 us
    all_gather x1, blocking collectives, on_device(): tables = lax.all_gather(table.reshape(params * columns, cam_width), CAM)  14.6 us
    all_to_all x2, waiting for transfers between devices, exchange(): lax.all_to_all(parts, axes, split_axis=0, concat_axis=0, tiled=True, axis...  12 us
    pallas_call x7, Pallas kernels, call(): pl.pallas_call(kernel, out_shape=tuple((jax.ShapeDtypeStruct(s, d) for s,...  8.88 us
  transfers between devices with their start and end apart: 2, of which 1 were waited for; matrix products, arithmetic and copies ran while one was open for 0% of the time, Pallas kernels for 1%

profile of v5, /device:TPU:1, one launch (start us, length us, event | category | flops | bytes accessed | tf_op | source)
XLA Modules:
  0.0 112.6 jit_solution(10415126843134969822)
XLA Ops:
  0.6 2.1 %shard_map.94 = (bf16[1024,128]{1,0:T(8,128)(2,1)}, s32[1,512]{1,0:T(1,128)S(1)}, bf16[128,512]{1,0:T(8,128)(2,1)S(1)}) custom-call(s32[1,512]{1,0:T(1,128)} %bitcast.34, s32[1,512]{1,0:T(1,128)} %bitcast.35, bf16[9,3,512]{2,1,0:T(4,128)(2,1)} %w_hbm.1), custom_call_target="tpu_custom_call" | custom-call | tf_op jit(solution)/shard_map/pallas_call | solution.py:34
  2.8 0.0 copy-start
  2.8 20.3 %all-to-all-start = ((bf16[64,16,128]{2,1,0:T(8,128)(2,1)}), bf16[64,16,128]{2,1,0:T(8,128)(2,1)S(1)}, u32[]{:S(2)}, u32[]{:S(2)}) async-start(bf16[64,16,128]{2,1,0:T(8,128)(2,1)} %bitcast.2), calls=%async_computation | async-start | bytes 524288 | tf_op jit(solution)/shard_map/all_to_all | solution.py:242
  23.1 0.0 copy-done
  23.1 14.6 %all_gather.3.table_ref = bf16[8,288,128]{2,1,0:T(8,128)(2,1)S(1)} all-gather(bf16[1,288,128]{2,1,0:T(8,128)(2,1)S(1)} %bitcast.28), channel_id=1, replica_groups=mesh['track_0'=8,'track_1'=8,'cam_0'=4,'cam_1'=2] {'cam_0','cam_1'}, dimensions={0}, use_global_device_ids=true | all-gather | bytes 663552 | tf_op jit(solution)/shard_map/all_gather | solution.py:265
  37.7 0.0 all-to-all-done
  37.7 1.4 %shard_map.95 = bf16[1024,128]{1,0:T(8,128)(2,1)} custom-call(bf16[1024,128]{1,0:T(8,128)(2,1)S(1)} %bitcast.23, bf16[8,288,128]{2,1,0:T(8,128)(2,1)S(1)} %all_gather.3.table_ref), custom_call_target="tpu_custom_call" | custom-call | tf_op jit(solution)/shard_map/pallas_call | solution.py:34
  39.1 4.6 %all-to-all-start.1 = ((bf16[64,16,128]{2,1,0:T(8,128)(2,1)}), bf16[64,16,128]{2,1,0:T(8,128)(2,1)S(1)}, u32[]{:S(2)}, u32[]{:S(2)}) async-start(bf16[64,16,128]{2,1,0:T(8,128)(2,1)} %bitcast.6), calls=%async_computation.1 | async-start | bytes 524288 | tf_op jit(solution)/shard_map/all_to_all | solution.py:242
  43.7 0.0 copy-start.4
  43.7 0.7 copy-done.4
  44.4 0.9 shard_map.96
  45.3 0.0 copy-start.3
  45.4 12.0 %all-to-all-done.1 = bf16[64,16,128]{2,1,0:T(8,128)(2,1)S(1)} async-done(((bf16[64,16,128]{2,1,0:T(8,128)(2,1)}), bf16[64,16,128]{2,1,0:T(8,128)(2,1)S(1)}, u32[]{:S(2)}, u32[]{:S(2)}) %all-to-all-start.1) | async-done | bytes 262176 | tf_op jit(solution)/shard_map/all_to_all | solution.py:242
  57.3 0.0 copy-done.3
  57.3 0.5 shard_map.97
  57.8 0.0 copy-start.2
  57.8 28.1 %all_to_all.25 = bf16[512,2,128]{2,1,0:T(2,128)(2,1)S(1)} all-to-all(bf16[512,2,128]{2,1,0:T(2,128)(2,1)S(1)} %bitcast.24), channel_id=1, replica_groups=mesh['track_0'=8,'track_1'=8,'cam_0'=4,'cam_1'=2] {'track_0','track_1','..., dimensions={0} | all-to-all | bytes 524288 | tf_op jit(solution)/shard_map/all_to_all | solution.py:242
  86.0 0.0 copy-done.2
  86.0 1.4 %shard_map.98 = (f32[9,32,128]{2,1,0:T(8,128)}, f32[16,8,128]{2,1,0:T(8,128)S(1)}) custom-call(bf16[1024,128]{1,0:T(8,128)(2,1)S(1)} %bitcast.25, bf16[9,32,128]{2,1,0:T(8,128)(2,1)S(1)} %bitcast.29, f32[9,9,128]{2,1,0:T(8,128)S(1)} %copy-done.2), custom_call_target="tpu_custom_call" | custom-call | tf_op jit(solution)/shard_map/pallas_call | solution.py:34
  87.4 9.6 %all_to_all.26 = f32[16,1,8,128]{3,2,1,0:T(8,128)S(1)} all-to-all(f32[16,1,8,128]{3,2,1,0:T(8,128)S(1)} %bitcast.32), channel_id=1, replica_groups={{32,1,8,9,16,17,24,25,0,33,40,41,48,49,56,57},{34,3,10,11,18,19,26,27,2..., dimensions={0} | all-to-all | bytes 131072 | tf_op jit(solution)/shard_map/all_to_all | solution.py:242
  97.0 0.0 copy-start.1
  97.0 13.1 %all_to_all.27 = f32[32,1,8,128]{3,2,1,0:T(8,128)S(1)} all-to-all(f32[32,1,8,128]{3,2,1,0:T(8,128)S(1)} %bitcast.27), channel_id=1, replica_groups={{260,2,4,6,64,66,68,70,128,130,132,134,192,194,196,198,256,258,0,262,32..., dimensions={0} | all-to-all | bytes 262144 | tf_op jit(solution)/shard_map/all_to_all | solution.py:242
  110.1 0.0 copy-done.1
  110.1 2.5 %shard_map.100 = (f32[9,32,128]{2,1,0:T(8,128)}, f32[32,32]{1,0:T(8,128)}) custom-call(f32[32,8,128]{2,1,0:T(8,128)S(1)} %bitcast.26, f32[9,32,128]{2,1,0:T(8,128)S(1)} %copy-done.1), custom_call_target="tpu_custom_call" | custom-call | tf_op jit(solution)/shard_map/pallas_call | solution.py:34
  (1 shorter events, 0.0 us)
Async XLA Ops:
  2.8 20.3 %copy-start = (bf16[32,9,128]{2,0,1:T(8,128)(2,1)S(1)}, bf16[32,9,128]{2,0,1:T(8,128)(2,1)}, u32[]{:S(2)}) copy-start(bf16[32,9,128]{2,0,1:T(8,128)(2,1)} %param.7) | copy-start | bytes 221188
  2.8 34.9 %all-to-all-start = ((bf16[64,16,128]{2,1,0:T(8,128)(2,1)}), bf16[64,16,128]{2,1,0:T(8,128)(2,1)S(1)}, u32[]{:S(2)}, u32[]{:S(2)}) async-start(bf16[64,16,128]{2,1,0:T(8,128)(2,1)} %bitcast.2), calls=%async_computation | async-start | bytes 524288 | tf_op jit(solution)/shard_map/all_to_all | solution.py:242
  39.1 18.2 %all-to-all-start.1 = ((bf16[64,16,128]{2,1,0:T(8,128)(2,1)}), bf16[64,16,128]{2,1,0:T(8,128)(2,1)S(1)}, u32[]{:S(2)}, u32[]{:S(2)}) async-start(bf16[64,16,128]{2,1,0:T(8,128)(2,1)} %bitcast.6), calls=%async_computation.1 | async-start | bytes 524288 | tf_op jit(solution)/shard_map/all_to_all | solution.py:242
  43.7 0.7 copy-start.4
  45.3 12.0 %copy-start.3 = (f32[3,3,128]{2,1,0:T(4,128)S(1)}, f32[3,3,128]{2,1,0:T(4,128)}, u32[]{:S(2)}) copy-start(f32[3,3,128]{2,1,0:T(4,128)} %v_ref.1) | copy-start | bytes 13828
  57.8 28.1 %copy-start.2 = (f32[9,9,128]{2,1,0:T(8,128)S(1)}, f32[9,9,128]{2,1,0:T(8,128)}, u32[]{:S(2)}) copy-start(f32[9,9,128]{2,1,0:T(8,128)} %u_ref.1) | copy-start | bytes 124420
  97.0 13.1 %copy-start.1 = (f32[9,32,128]{2,1,0:T(8,128)S(1)}, f32[9,32,128]{2,1,0:T(8,128)}, u32[]{:S(2)}) copy-start(f32[9,32,128]{2,1,0:T(8,128)} %get-tuple-element.19.sketch_ref) | copy-start | bytes 442372

commit v6 on v5

--- a/solution.py
+++ b/solution.py
@@ -45,12 +45,14 @@
     camera_hbm,
     mask_hbm,
     w_hbm,
+    track_hbm,
     request_ref,
     slot_ref,
     values_ref,
     camera_ref,
     mask_ref,
     w_ref,
+    track_ref,
     rows,
     sems,
 ):
@@ -58,7 +60,7 @@
     copies = [
         pltpu.make_async_copy(source, target, sems.at[n])
         for n, (source, target) in enumerate(
-            ((camera_hbm, camera_ref), (mask_hbm, mask_ref), (w_hbm, w_ref))
+            ((camera_hbm, camera_ref), (mask_hbm, mask_ref), (w_hbm, w_ref), (track_hbm, track_ref))
         )
     ]
     for copy in copies:
@@ -82,7 +84,8 @@
             same = same + jnp.where(column_of[b] == row_of[q], 1.0, 0.0)
         ranks.append(jnp.sum(same, axis=0, keepdims=True))
     slot = owner * capacity + jnp.concatenate(ranks, axis=1).astype(jnp.int32)
-    slot_ref[...] = slot
+    slot_ref[0:1, :] = slot
+    slot_ref[1:2, :] = track_ref[...]
     at_head = (slot >= head) & (slot < head + block)
     slot = jnp.where(slot < block, slot + head, jnp.where(at_head, slot - head, slot))
     live = mask_ref[...].astype(F32)
@@ -99,17 +102,17 @@
         request_ref[s : s + step, :] = dot_lanes(chosen, values).astype(BF16)
 
 
-def member_kernel(slot_ref, track_ref, values_ref, by_track_ref, by_slot_ref, base_ref):
+def member_kernel(slot_ref, values_ref, by_track_ref, by_slot_ref, base_ref):
     obs = slot_ref.shape[1]
     tracks, slots = by_track_ref.shape
     position = lax.broadcasted_iota(jnp.int32, (1, obs), 1)
-    track = lax.shift_right_logical(position, 7) * TRK_BLK + track_ref[...]
+    track = lax.shift_right_logical(position, 7) * TRK_BLK + slot_ref[1:2, :]
     ids = lax.broadcasted_iota(jnp.int32, (tracks, obs), 0)
     member = jnp.where(ids == track, 1.0, 0.0).astype(BF16)
     step = 256
     for s in range(0, slots, step):
         ids = lax.broadcasted_iota(jnp.int32, (step, obs), 0) + s
-        chosen = jnp.where(ids == slot_ref[...], 1.0, 0.0).astype(BF16)
+        chosen = jnp.where(ids == slot_ref[0:1, :], 1.0, 0.0).astype(BF16)
         by_track_ref[:, s : s + step] = dot_lanes(member, chosen).astype(BF16)
         by_slot_ref[s : s + step, :] = dot_lanes(chosen, member).astype(BF16)
         base_ref[s : s + step, :] = dot_lanes(chosen, values_ref[...]).astype(BF16)
@@ -147,7 +150,10 @@
     reply_ref[head : head + block, :] = out_rows[0:block, :].astype(BF16)
 
 
-def solve_kernel(reply_ref, by_track_ref, by_slot_ref, v_ref, base_ref, out_ref):
+def solve_kernel(
+    reply_ref, slot_ref, values_ref, v_ref, out_ref, by_track_ref, by_slot_ref, base_ref
+):
+    member_kernel(slot_ref, values_ref, by_track_ref, by_slot_ref, base_ref)
     summed = dot(by_track_ref[...], reply_ref[...]).T
     parts = []
     for i in range(3):
@@ -268,19 +274,25 @@
     block = cam_count * capacity
     request, slot, values = call(
         functools.partial(request_kernel, (capacity, head * block, block)),
-        (by_slot_shape, ((1, obs), jnp.int32), ((LANES, obs), BF16)),
+        (by_slot_shape, ((2, obs), jnp.int32), ((LANES, obs), BF16)),
         *(
             pltpu.with_memory_space_constraint(x, pltpu.HBM)
-            for x in (obs_camera.reshape(1, obs), obs_mask.reshape(1, obs), w_blocks)
+            for x in (
+                obs_camera.reshape(1, obs),
+                obs_mask.reshape(1, obs),
+                w_blocks,
+                obs_track.reshape(1, obs),
+            )
         ),
         scratch=(
             pltpu.VMEM((1, obs), jnp.int32),
             pltpu.VMEM((1, obs), jnp.int32),
             pltpu.VMEM(w_blocks.shape, BF16),
+            pltpu.VMEM((1, obs), jnp.int32),
             pltpu.VMEM((LANES, obs), F32),
-            pltpu.SemaphoreType.DMA((3,)),
+            pltpu.SemaphoreType.DMA((4,)),
         ),
-        in_specs=[pl.BlockSpec(memory_space=pltpu.HBM)] * 3,
+        in_specs=[pl.BlockSpec(memory_space=pltpu.HBM)] * 4,
     )
     asked = exchange(request, TRACK, head)
     (reply,) = call(
@@ -292,15 +304,18 @@
     )
     projected = exchange(reply, TRACK)
 
-    by_track, by_slot, base = call(
-        member_kernel,
-        (((tracks, slots), BF16), ((slots, tracks), BF16), by_slot_shape),
+    (outgoing,) = call(
+        solve_kernel,
+        (by_slot_shape,),
+        projected,
         slot,
-        obs_track.reshape(1, obs),
         values,
-    )
-    (outgoing,) = call(
-        solve_kernel, (by_slot_shape,), projected, by_track, by_slot, v_inverse, base
+        v_inverse,
+        scratch=(
+            pltpu.VMEM((tracks, slots), BF16),
+            pltpu.VMEM((slots, tracks), BF16),
+            pltpu.VMEM((slots, LANES), BF16),
+        ),
     )
     solved = exchange(outgoing, TRACK_CAM)
 

time: 113 us -> 112 us (level)
  blocking collectives: 65.4 us -> 82.9 us
  waiting for transfers between devices: 12 us -> 0.01 us
  starting transfers between devices: 24.9 us -> 20.3 us
    all_to_all x3 -> x4, blocking collectives: 50.8 us -> 68.2 us  [exchange(): lax.all_to_all(parts, axes, split_axis=0, concat_axis=0, tiled=True, axis...]
    all_to_all x2 -> x1, waiting for transfers between devices: 12 us -> 0.01 us  [exchange(): lax.all_to_all(parts, axes, split_axis=0, concat_axis=0, tiled=True, axis...]
    all_to_all x2 -> x1, starting transfers between devices: 24.9 us -> 20.3 us  [exchange(): lax.all_to_all(parts, axes, split_axis=0, concat_axis=0, tiled=True, axis...]
    pallas_call x7 -> x6, Pallas kernels: 8.88 us -> 8.12 us  [call(): pl.pallas_call(kernel, out_shape=tuple((jax.ShapeDtypeStruct(s, d) for s,...]
  transfers between devices with their start and end apart: 2 -> 1, of which waited for: 1 -> 0; matrix products, arithmetic and copies ran while one was open for 0% -> 0% of each run, Pallas kernels for 1% -> 0%
where the time goes in v6:
time: 112 us
  blocking collectives  82.9 us (74%)
  starting transfers between devices  20.3 us (18%)
  Pallas kernels  8.12 us (7%)
    all_to_all x4, blocking collectives, exchange(): lax.all_to_all(parts, axes, split_axis=0, concat_axis=0, tiled=True, axis...  68.2 us
    all_to_all x1, starting transfers between devices, exchange(): lax.all_to_all(parts, axes, split_axis=0, concat_axis=0, tiled=True, axis...  20.3 us
    all_gather x1, blocking collectives, on_device(): tables = lax.all_gather(table.reshape(params * columns, cam_width), CAM)  14.6 us
    pallas_call x6, Pallas kernels, call(): pl.pallas_call(kernel, out_shape=tuple((jax.ShapeDtypeStruct(s, d) for s,...  8.12 us
  transfers between devices with their start and end apart: 1, of which 0 were waited for; matrix products, arithmetic and copies ran while one was open for 0% of the time, Pallas kernels for 0%

profile of v6, /device:TPU:1, one launch (start us, length us, event | category | flops | bytes accessed | tf_op | source)
XLA Modules:
  0.0 112.0 jit_solution(3616840706187955837)
XLA Ops:
  0.6 2.1 %shard_map.94 = (bf16[1024,128]{1,0:T(8,128)(2,1)}, s32[2,512]{1,0:T(2,128)S(1)}, bf16[128,512]{1,0:T(8,128)(2,1)S(1)}) custom-call(s32[1,512]{1,0:T(1,128)} %bitcast.34, s32[1,512]{1,0:T(1,128)} %bitcast.35, bf16[9,3,512]{2,1,0:T(4,128)(2,1)} %w_hbm.1, s32[1,512]{1,0:T(1,128)} %bitcast.36), custom_call_target="tpu_custom_call" | custom-call | tf_op jit(solution)/shard_map/pallas_call | solution.py:34
  2.8 0.0 copy-start
  2.8 20.3 %all-to-all-start = ((bf16[64,16,128]{2,1,0:T(8,128)(2,1)}), bf16[64,16,128]{2,1,0:T(8,128)(2,1)S(1)}, u32[]{:S(2)}, u32[]{:S(2)}) async-start(bf16[64,16,128]{2,1,0:T(8,128)(2,1)} %bitcast.3), calls=%async_computation | async-start | bytes 524288 | tf_op jit(solution)/shard_map/all_to_all | solution.py:248
  23.1 0.0 copy-done
  23.1 14.6 %all_gather.3.table_ref = bf16[8,288,128]{2,1,0:T(8,128)(2,1)S(1)} all-gather(bf16[1,288,128]{2,1,0:T(8,128)(2,1)S(1)} %bitcast.29), channel_id=1, replica_groups=mesh['track_0'=8,'track_1'=8,'cam_0'=4,'cam_1'=2] {'cam_0','cam_1'}, dimensions={0}, use_global_device_ids=true | all-gather | bytes 663552 | tf_op jit(solution)/shard_map/all_gather | solution.py:271
  37.7 0.0 all-to-all-done
  37.7 0.7 shard_map.95
  38.4 0.0 copy-start.3
  38.4 17.4 %all_to_all.25 = bf16[64,16,128]{2,1,0:T(8,128)(2,1)S(1)} all-to-all(bf16[64,16,128]{2,1,0:T(8,128)(2,1)S(1)} %bitcast.23), channel_id=1, replica_groups=mesh['track_0'=8,'track_1'=8,'cam_0'=4,'cam_1'=2] {'track_0','track_1'}, dimensions={0} | all-to-all | bytes 524288 | tf_op jit(solution)/shard_map/all_to_all | solution.py:248
  55.8 0.0 copy-done.3
  55.8 1.4 %shard_map.96 = bf16[1024,128]{1,0:T(8,128)(2,1)S(1)} custom-call(bf16[1024,128]{1,0:T(8,128)(2,1)S(1)} %bitcast.25, s32[2,512]{1,0:T(2,128)S(1)} %get-tuple-element.11.slot_ref, bf16[128,512]{1,0:T(8,128)(2,1)S(1)} %get-tuple-element.12.values_ref, f32[3,3,128]{2,1,0:T(4,128)S(1)} %copy-done.3), custom_call_target="tpu_custom_call" | custom-call | tf_op jit(solution)/shard_map/pallas_call | solution.py:34
  57.2 0.0 copy-start.2
  57.2 28.1 %all_to_all.26 = bf16[512,2,128]{2,1,0:T(2,128)(2,1)S(1)} all-to-all(bf16[512,2,128]{2,1,0:T(2,128)(2,1)S(1)} %bitcast.26), channel_id=1, replica_groups=mesh['track_0'=8,'track_1'=8,'cam_0'=4,'cam_1'=2] {'track_0','track_1','..., dimensions={0} | all-to-all | bytes 524288 | tf_op jit(solution)/shard_map/all_to_all | solution.py:248
  85.4 0.0 copy-done.2
  85.4 1.4 %shard_map.97 = (f32[9,32,128]{2,1,0:T(8,128)}, f32[16,8,128]{2,1,0:T(8,128)S(1)}) custom-call(bf16[1024,128]{1,0:T(8,128)(2,1)S(1)} %bitcast.24, bf16[9,32,128]{2,1,0:T(8,128)(2,1)S(1)} %bitcast.30, f32[9,9,128]{2,1,0:T(8,128)S(1)} %copy-done.2), custom_call_target="tpu_custom_call" | custom-call | tf_op jit(solution)/shard_map/pallas_call | solution.py:34
  86.8 9.6 %all_to_all.27 = f32[16,1,8,128]{3,2,1,0:T(8,128)S(1)} all-to-all(f32[16,1,8,128]{3,2,1,0:T(8,128)S(1)} %bitcast.33), channel_id=1, replica_groups={{32,1,8,9,16,17,24,25,0,33,40,41,48,49,56,57},{34,3,10,11,18,19,26,27,2..., dimensions={0} | all-to-all | bytes 131072 | tf_op jit(solution)/shard_map/all_to_all | solution.py:248
  96.4 0.0 copy-start.1
  96.4 13.1 %all_to_all.28 = f32[32,1,8,128]{3,2,1,0:T(8,128)S(1)} all-to-all(f32[32,1,8,128]{3,2,1,0:T(8,128)S(1)} %bitcast.28), channel_id=1, replica_groups={{260,2,4,6,64,66,68,70,128,130,132,134,192,194,196,198,256,258,0,262,32..., dimensions={0} | all-to-all | bytes 262144 | tf_op jit(solution)/shard_map/all_to_all | solution.py:248
  109.5 0.0 copy-done.1
  109.5 2.5 %shard_map.99 = (f32[9,32,128]{2,1,0:T(8,128)}, f32[32,32]{1,0:T(8,128)}) custom-call(f32[32,8,128]{2,1,0:T(8,128)S(1)} %bitcast.27, f32[9,32,128]{2,1,0:T(8,128)S(1)} %copy-done.1), custom_call_target="tpu_custom_call" | custom-call | tf_op jit(solution)/shard_map/pallas_call | solution.py:34
  (1 shorter events, 0.0 us)
Async XLA Ops:
  2.8 20.3 %copy-start = (bf16[32,9,128]{2,0,1:T(8,128)(2,1)S(1)}, bf16[32,9,128]{2,0,1:T(8,128)(2,1)}, u32[]{:S(2)}) copy-start(bf16[32,9,128]{2,0,1:T(8,128)(2,1)} %param.7) | copy-start | bytes 221188
  2.8 34.9 %all-to-all-start = ((bf16[64,16,128]{2,1,0:T(8,128)(2,1)}), bf16[64,16,128]{2,1,0:T(8,128)(2,1)S(1)}, u32[]{:S(2)}, u32[]{:S(2)}) async-start(bf16[64,16,128]{2,1,0:T(8,128)(2,1)} %bitcast.3), calls=%async_computation | async-start | bytes 524288 | tf_op jit(solution)/shard_map/all_to_all | solution.py:248
  38.4 17.4 %copy-start.3 = (f32[3,3,128]{2,1,0:T(4,128)S(1)}, f32[3,3,128]{2,1,0:T(4,128)}, u32[]{:S(2)}) copy-start(f32[3,3,128]{2,1,0:T(4,128)} %v_ref.1) | copy-start | bytes 13828
  57.2 28.2 %copy-start.2 = (f32[9,9,128]{2,1,0:T(8,128)S(1)}, f32[9,9,128]{2,1,0:T(8,128)}, u32[]{:S(2)}) copy-start(f32[9,9,128]{2,1,0:T(8,128)} %u_ref.1) | copy-start | bytes 124420
  96.4 13.1 %copy-start.1 = (f32[9,32,128]{2,1,0:T(8,128)S(1)}, f32[9,32,128]{2,1,0:T(8,128)}, u32[]{:S(2)}) copy-start(f32[9,32,128]{2,1,0:T(8,128)} %get-tuple-element.13.sketch_ref) | copy-start | bytes 442372

commit v7 on v6

--- a/solution.py
+++ b/solution.py
@@ -122,6 +122,13 @@
     return jnp.dot(lhs, rhs, preferred_element_type=F32)
 
 
+def three_parts(values):
+    top = values.astype(BF16)
+    rest = values - top.astype(F32)
+    second = rest.astype(BF16)
+    return [top, second, (rest - second.astype(F32)).astype(BF16)]
+
+
 def project_kernel(sizes, request_ref, table_ref, reply_ref, rows, out_rows):
     capacity, head, block = sizes
     cams = table_ref.shape[0]
@@ -199,9 +206,11 @@
         parts.append(own[m] - (summed[at : at + COLS, :] + summed[half + at : half + at + COLS, :]))
         sketch_ref[m] = parts[m]
     wide = jnp.concatenate(parts, axis=1)
-    gram = lax.dot_general(
-        wide, wide, (((1,), (1,)), ((), ())), precision=HIGH, preferred_element_type=F32
-    )
+    stacked = jnp.concatenate(three_parts(wide), axis=0)
+    products = dot_lanes(stacked, stacked)
+    gram = jnp.zeros((COLS, COLS), F32)
+    for p, q in ((2, 2), (1, 2), (2, 1), (0, 2), (1, 1), (2, 0), (0, 1), (1, 0), (0, 0)):
+        gram = gram + products[COLS * p : COLS * (p + 1), COLS * q : COLS * (q + 1)]
     packed = jnp.concatenate([gram[8 * q : 8 * q + 8, :] for q in range(4)], axis=1)
     gram_ref[...] = jnp.broadcast_to(packed[None], gram_ref.shape)
 

time: 112 us -> 112 us (level)
  no operation moved by 1% of the time
where the time goes in v7:
time: 112 us
  blocking collectives  82.9 us (74%)
  starting transfers between devices  20.3 us (18%)
  Pallas kernels  8.08 us (7%)
    all_to_all x4, blocking collectives, exchange(): lax.all_to_all(parts, axes, split_axis=0, concat_axis=0, tiled=True, axis...  68.2 us
    all_to_all x1, starting transfers between devices, exchange(): lax.all_to_all(parts, axes, split_axis=0, concat_axis=0, tiled=True, axis...  20.3 us
    all_gather x1, blocking collectives, on_device(): tables = lax.all_gather(table.reshape(params * columns, cam_width), CAM)  14.6 us
    pallas_call x6, Pallas kernels, call(): pl.pallas_call(kernel, out_shape=tuple((jax.ShapeDtypeStruct(s, d) for s,...  8.08 us
  transfers between devices with their start and end apart: 1, of which 0 were waited for; matrix products, arithmetic and copies ran while one was open for 0% of the time, Pallas kernels for 0%

profile of v7, /device:TPU:1, one launch (start us, length us, event | category | flops | bytes accessed | tf_op | source)
XLA Modules:
  0.0 111.9 jit_solution(18267361001364727152)
XLA Ops:
  0.6 2.1 %shard_map.94 = (bf16[1024,128]{1,0:T(8,128)(2,1)}, s32[2,512]{1,0:T(2,128)S(1)}, bf16[128,512]{1,0:T(8,128)(2,1)S(1)}) custom-call(s32[1,512]{1,0:T(1,128)} %bitcast.34, s32[1,512]{1,0:T(1,128)} %bitcast.35, bf16[9,3,512]{2,1,0:T(4,128)(2,1)} %w_hbm.1, s32[1,512]{1,0:T(1,128)} %bitcast.36), custom_call_target="tpu_custom_call" | custom-call | tf_op jit(solution)/shard_map/pallas_call | solution.py:34
  2.8 0.0 copy-start
  2.8 20.3 %all-to-all-start = ((bf16[64,16,128]{2,1,0:T(8,128)(2,1)}), bf16[64,16,128]{2,1,0:T(8,128)(2,1)S(1)}, u32[]{:S(2)}, u32[]{:S(2)}) async-start(bf16[64,16,128]{2,1,0:T(8,128)(2,1)} %bitcast.3), calls=%async_computation | async-start | bytes 524288 | tf_op jit(solution)/shard_map/all_to_all | solution.py:257
  23.1 0.0 copy-done
  23.1 14.6 %all_gather.3.table_ref = bf16[8,288,128]{2,1,0:T(8,128)(2,1)S(1)} all-gather(bf16[1,288,128]{2,1,0:T(8,128)(2,1)S(1)} %bitcast.29), channel_id=1, replica_groups=mesh['track_0'=8,'track_1'=8,'cam_0'=4,'cam_1'=2] {'cam_0','cam_1'}, dimensions={0}, use_global_device_ids=true | all-gather | bytes 663552 | tf_op jit(solution)/shard_map/all_gather | solution.py:280
  37.7 0.0 all-to-all-done
  37.7 0.7 shard_map.95
  38.4 0.0 copy-start.3
  38.4 17.4 %all_to_all.25 = bf16[64,16,128]{2,1,0:T(8,128)(2,1)S(1)} all-to-all(bf16[64,16,128]{2,1,0:T(8,128)(2,1)S(1)} %bitcast.23), channel_id=1, replica_groups=mesh['track_0'=8,'track_1'=8,'cam_0'=4,'cam_1'=2] {'track_0','track_1'}, dimensions={0} | all-to-all | bytes 524288 | tf_op jit(solution)/shard_map/all_to_all | solution.py:257
  55.8 0.0 copy-done.3
  55.8 1.4 %shard_map.96 = bf16[1024,128]{1,0:T(8,128)(2,1)S(1)} custom-call(bf16[1024,128]{1,0:T(8,128)(2,1)S(1)} %bitcast.25, s32[2,512]{1,0:T(2,128)S(1)} %get-tuple-element.11.slot_ref, bf16[128,512]{1,0:T(8,128)(2,1)S(1)} %get-tuple-element.12.values_ref, f32[3,3,128]{2,1,0:T(4,128)S(1)} %copy-done.3), custom_call_target="tpu_custom_call" | custom-call | tf_op jit(solution)/shard_map/pallas_call | solution.py:34
  57.2 0.0 copy-start.2
  57.2 28.1 %all_to_all.26 = bf16[512,2,128]{2,1,0:T(2,128)(2,1)S(1)} all-to-all(bf16[512,2,128]{2,1,0:T(2,128)(2,1)S(1)} %bitcast.26), channel_id=1, replica_groups=mesh['track_0'=8,'track_1'=8,'cam_0'=4,'cam_1'=2] {'track_0','track_1','..., dimensions={0} | all-to-all | bytes 524288 | tf_op jit(solution)/shard_map/all_to_all | solution.py:257
  85.4 0.0 copy-done.2
  85.4 1.3 %shard_map.97 = (f32[9,32,128]{2,1,0:T(8,128)}, f32[16,8,128]{2,1,0:T(8,128)S(1)}) custom-call(bf16[1024,128]{1,0:T(8,128)(2,1)S(1)} %bitcast.24, bf16[9,32,128]{2,1,0:T(8,128)(2,1)S(1)} %bitcast.30, f32[9,9,128]{2,1,0:T(8,128)S(1)} %copy-done.2), custom_call_target="tpu_custom_call" | custom-call | tf_op jit(solution)/shard_map/pallas_call | solution.py:34
  86.7 9.6 %all_to_all.27 = f32[16,1,8,128]{3,2,1,0:T(8,128)S(1)} all-to-all(f32[16,1,8,128]{3,2,1,0:T(8,128)S(1)} %bitcast.33), channel_id=1, replica_groups={{32,1,8,9,16,17,24,25,0,33,40,41,48,49,56,57},{34,3,10,11,18,19,26,27,2..., dimensions={0} | all-to-all | bytes 131072 | tf_op jit(solution)/shard_map/all_to_all | solution.py:257
  96.4 0.0 copy-start.1
  96.4 13.1 %all_to_all.28 = f32[32,1,8,128]{3,2,1,0:T(8,128)S(1)} all-to-all(f32[32,1,8,128]{3,2,1,0:T(8,128)S(1)} %bitcast.28), channel_id=1, replica_groups={{260,2,4,6,64,66,68,70,128,130,132,134,192,194,196,198,256,258,0,262,32..., dimensions={0} | all-to-all | bytes 262144 | tf_op jit(solution)/shard_map/all_to_all | solution.py:257
  109.5 0.0 copy-done.1
  109.5 2.5 %shard_map.99 = (f32[9,32,128]{2,1,0:T(8,128)}, f32[32,32]{1,0:T(8,128)}) custom-call(f32[32,8,128]{2,1,0:T(8,128)S(1)} %bitcast.27, f32[9,32,128]{2,1,0:T(8,128)S(1)} %copy-done.1), custom_call_target="tpu_custom_call" | custom-call | tf_op jit(solution)/shard_map/pallas_call | solution.py:34
  (1 shorter events, 0.0 us)
Async XLA Ops:
  2.8 20.3 %copy-start = (bf16[32,9,128]{2,0,1:T(8,128)(2,1)S(1)}, bf16[32,9,128]{2,0,1:T(8,128)(2,1)}, u32[]{:S(2)}) copy-start(bf16[32,9,128]{2,0,1:T(8,128)(2,1)} %param.7) | copy-start | bytes 221188
  2.8 34.9 %all-to-all-start = ((bf16[64,16,128]{2,1,0:T(8,128)(2,1)}), bf16[64,16,128]{2,1,0:T(8,128)(2,1)S(1)}, u32[]{:S(2)}, u32[]{:S(2)}) async-start(bf16[64,16,128]{2,1,0:T(8,128)(2,1)} %bitcast.3), calls=%async_computation | async-start | bytes 524288 | tf_op jit(solution)/shard_map/all_to_all | solution.py:257
  38.4 17.4 %copy-start.3 = (f32[3,3,128]{2,1,0:T(4,128)S(1)}, f32[3,3,128]{2,1,0:T(4,128)}, u32[]{:S(2)}) copy-start(f32[3,3,128]{2,1,0:T(4,128)} %v_ref.1) | copy-start | bytes 13828
  57.2 28.2 %copy-start.2 = (f32[9,9,128]{2,1,0:T(8,128)S(1)}, f32[9,9,128]{2,1,0:T(8,128)}, u32[]{:S(2)}) copy-start(f32[9,9,128]{2,1,0:T(8,128)} %u_ref.1) | copy-start | bytes 124420
  96.4 13.1 %copy-start.1 = (f32[9,32,128]{2,1,0:T(8,128)S(1)}, f32[9,32,128]{2,1,0:T(8,128)}, u32[]{:S(2)}) copy-start(f32[9,32,128]{2,1,0:T(8,128)} %get-tuple-element.13.sketch_ref) | copy-start | bytes 442372
